TPU v7x, 32 devices: a whole 2x2x4 slice. The times are simulated.
32 devices in a mesh: dp: 16 (over z, y, x), mp: 2 (over core).
Axes of the slice: x: 2, y: 2, z: 4, core: 2. Of those that a mesh axis runs over, the one named last changes fastest.
Arguments:
- x_rows: bfloat16 [24576, 384], P(('dp', 'mp')), may hold values from -6 to 6
- cotangent: float32 [24576, 384], P(('dp', 'mp')), may hold values from -12 to 12
- task_ids: int32 [16], P('dp'), may hold values from 0 to 4
- routes: int32 [24576, 4], P('dp'), may hold values from 0 to 7, all different within a row; in each aligned block of 1536 rows (0 to 1535, 1536 to 3071, ...) at most 1536 rows name the same one
- norm_params: float32 [4, 384], replicated, may hold values from -0.4 to 3
- norm_first: float32 [4, 384], replicated, may hold values from -0.00390625 to 0.00390625
- norm_second: float32 [4, 384], replicated, may hold values from 6.3861902e-09 to 2.5544761e-08
- norm_ema: float32 [4, 384], replicated, may hold values from -0.4 to 2
- qkv_weight: float32 [3, 384, 384], P(None, 'dp', 'mp'), may hold values from -0.3125 to 0.3125
- qkv_first: float32 [3, 384, 384], P(None, 'dp', 'mp'), may hold values from -0.001953125 to 0.001953125
- qkv_second: float32 [3, 384, 384], P(None, 'dp', 'mp'), may hold values from 1.5965476e-09 to 6.3861902e-09
- qkv_ema: float32 [3, 384, 384], P(None, 'dp', 'mp'), may hold values from -0.3125 to 0.3125
- out_weight: float32 [384, 384], P('dp', 'mp'), may hold values from -1.5 to 1.5
- out_first: float32 [384, 384], P('dp', 'mp'), may hold values from -0.0009765625 to 0.0009765625
- out_second: float32 [384, 384], P('dp', 'mp'), may hold values from 3.991369e-10 to 1.5965476e-09
- out_ema: float32 [384, 384], P('dp', 'mp'), may hold values from -1.5 to 1.5
- router: float32 [389, 8], replicated, may hold values from -2 to 2
- router_first: float32 [389, 8], replicated, may hold values from -0.00048828125 to 0.00048828125
- router_second: float32 [389, 8], replicated, may hold values from 9.978422e-11 to 3.991369e-10
- router_ema: float32 [389, 8], replicated, may hold values from -2 to 2
- expert_in: float32 [8, 384, 1536], P(None, 'dp', 'mp'), may hold values from -0.3125 to 0.3125
- expert_in_first: float32 [8, 384, 1536], P(None, 'dp', 'mp'), may hold values from -0.00024414062 to 0.00024414062
- expert_in_second: float32 [8, 384, 1536], P(None, 'dp', 'mp'), may hold values from 2.4946056e-11 to 9.978422e-11
- expert_in_ema: float32 [8, 384, 1536], P(None, 'dp', 'mp'), may hold values from -0.3125 to 0.3125
- expert_out: float32 [8, 384, 1536], P(None, 'dp', 'mp'), may hold values from -0.3125 to 0.3125
- expert_out_first: float32 [8, 384, 1536], P(None, 'dp', 'mp'), may hold values from -0.00061035156 to 0.00061035156
- expert_out_second: float32 [8, 384, 1536], P(None, 'dp', 'mp'), may hold values from 1.6863534e-10 to 6.7454137e-10
- expert_out_ema: float32 [8, 384, 1536], P(None, 'dp', 'mp'), may hold values from -0.3125 to 0.3125
Outputs:
- output: float32 [24576, 384], P(('dp', 'mp'))
- input_grad: float32 [24576, 384], P(('dp', 'mp'))
- grad_norm: float32 [1], replicated
- norm_params_new: float32 [4, 384], replicated
- norm_first_new: float32 [4, 384], replicated
- norm_second_new: float32 [4, 384], replicated
- norm_ema_new: float32 [4, 384], replicated
- qkv_weight_new: float32 [3, 384, 384], P(None, 'dp', 'mp')
- qkv_first_new: float32 [3, 384, 384], P(None, 'dp', 'mp')
- qkv_second_new: float32 [3, 384, 384], P(None, 'dp', 'mp')
- qkv_ema_new: float32 [3, 384, 384], P(None, 'dp', 'mp')
- out_weight_new: float32 [384, 384], P('dp', 'mp')
- out_first_new: float32 [384, 384], P('dp', 'mp')
- out_second_new: float32 [384, 384], P('dp', 'mp')
- out_ema_new: float32 [384, 384], P('dp', 'mp')
- router_new: float32 [389, 8], replicated
- router_first_new: float32 [389, 8], replicated
- router_second_new: float32 [389, 8], replicated
- router_ema_new: float32 [389, 8], replicated
- expert_in_new: float32 [8, 384, 1536], P(None, 'dp', 'mp')
- expert_in_first_new: float32 [8, 384, 1536], P(None, 'dp', 'mp')
- expert_in_second_new: float32 [8, 384, 1536], P(None, 'dp', 'mp')
- expert_in_ema_new: float32 [8, 384, 1536], P(None, 'dp', 'mp')
- expert_out_new: float32 [8, 384, 1536], P(None, 'dp', 'mp')
- expert_out_first_new: float32 [8, 384, 1536], P(None, 'dp', 'mp')
- expert_out_second_new: float32 [8, 384, 1536], P(None, 'dp', 'mp')
- expert_out_ema_new: float32 [8, 384, 1536], P(None, 'dp', 'mp')
Inputs may be any that keep to these rules, and one draw needn't show every extreme that they name: `routes`: each row names 4 different experts; within each aligned block of 1536 rows (the patches of one index of dp) no expert is named by more than 1536 rows.
All inputs are finite; a program needn't handle non-finite values.
Results may differ from a plain program's by a relative error of at most 0.02.
Values may be sent and summed in bfloat16 or wider, within the bound.
A program may use at most 192 MiB of HBM per device.

v0:
```python
import jax
import jax.numpy as jnp
from jax import lax
from jax.sharding import PartitionSpec as P

D = 384
HD = 64
E = 8
TOP = 4
TASKS = 5
L = 1536
STEP = 10
IMGS = 1
R = 1536
QB = 512
CAP = 1536


NORM_EPS = 1e-06
SCORE_SCALE = 0.125
CLIP_LIMIT = 1.0
BETA_FIRST = 0.9
BETA_SECOND = 0.999
LEARN_RATE = 0.1
NORM_RATE = 0.5
WEIGHT_DECAY = 0.05
ADAM_EPS = 1e-08
EMA_KEEP = 0.6
SQRT_HALF = 0.7071067811865476
INV_SQRT_TWO_PI = 0.3989422804014327


def norm_forward(rows, gain, shift):
    row_mean = jnp.mean(rows, axis=-1, keepdims=True)
    centered = rows - row_mean
    inv_std = lax.rsqrt(jnp.mean(centered * centered, axis=-1, keepdims=True) + NORM_EPS)
    unit = centered * inv_std
    return (unit * gain + shift, unit, inv_std)


def norm_backward(upstream, unit, inv_std, gain):
    scaled = upstream * gain
    inner = jnp.mean(scaled * unit, axis=-1, keepdims=True)
    grad_rows = inv_std * (scaled - jnp.mean(scaled, axis=-1, keepdims=True) - unit * inner)
    return (grad_rows, jnp.sum(upstream * unit, axis=0), jnp.sum(upstream, axis=0))


def gelu_exact(values):
    return 0.5 * values * (1.0 + lax.erf(values * SQRT_HALF))


def gelu_slope(values):
    return 0.5 * (1.0 + lax.erf(values * SQRT_HALF)) + values * INV_SQRT_TWO_PI * jnp.exp(
        -0.5 * values * values
    )


def dense_exact(left, right):
    return jnp.dot(left, right, precision=lax.Precision.HIGHEST, preferred_element_type=jnp.float32)


def slot_table(route_rows, experts, capacity):
    flat_routes = route_rows.reshape(-1)
    one_hot = (flat_routes[:, None] == jnp.arange(experts, dtype=jnp.int32)[None, :]).astype(
        jnp.int32
    )
    earlier = jnp.cumsum(one_hot, axis=0) - one_hot
    position = jnp.sum(earlier * one_hot, axis=1)
    return flat_routes * capacity + position


def attend_image(queries, keys_img, values_img, block_rows):
    blended_parts = []
    total_parts = []
    for offset in range(0, queries.shape[0], block_rows):
        query_block = queries[offset : offset + block_rows]
        scores = (
            jnp.einsum("qhd,khd->hqk", query_block, keys_img, preferred_element_type=jnp.float32)
            * SCORE_SCALE
        )
        row_peak = jnp.max(scores, axis=-1, keepdims=True)
        powers = jnp.exp(scores - row_peak)
        row_total = jnp.sum(powers, axis=-1, keepdims=True)
        probability = (powers / row_total).astype(jnp.bfloat16)
        blended = jnp.einsum(
            "hqk,khd->qhd", probability, values_img, preferred_element_type=jnp.float32
        )
        blended_parts.append(blended.astype(jnp.bfloat16))
        total_parts.append((row_peak + jnp.log(row_total))[:, :, 0])
    return (jnp.concatenate(blended_parts, axis=0), jnp.concatenate(total_parts, axis=1))


def attend_image_back(queries, keys_img, values_img, log_total, grad_context, block_rows):
    query_parts = []
    grad_keys = jnp.zeros(keys_img.shape, jnp.float32)
    grad_values = jnp.zeros(values_img.shape, jnp.float32)
    for offset in range(0, queries.shape[0], block_rows):
        query_block = queries[offset : offset + block_rows]
        grad_block = grad_context[offset : offset + block_rows]
        scores = (
            jnp.einsum("qhd,khd->hqk", query_block, keys_img, preferred_element_type=jnp.float32)
            * SCORE_SCALE
        )
        probability = jnp.exp(scores - log_total[:, offset : offset + block_rows, None])
        prob_low = probability.astype(jnp.bfloat16)
        grad_prob = jnp.einsum(
            "qhd,khd->hqk", grad_block, values_img, preferred_element_type=jnp.float32
        )
        inner = jnp.sum(probability * grad_prob, axis=-1, keepdims=True)
        grad_scores = (probability * (grad_prob - inner)).astype(jnp.bfloat16)
        query_parts.append(
            jnp.einsum("hqk,khd->qhd", grad_scores, keys_img, preferred_element_type=jnp.float32)
            * SCORE_SCALE
        )
        grad_keys = (
            grad_keys
            + jnp.einsum(
                "hqk,qhd->khd", grad_scores, query_block, preferred_element_type=jnp.float32
            )
            * SCORE_SCALE
        )
        grad_values = grad_values + jnp.einsum(
            "hqk,qhd->khd", prob_low, grad_block, preferred_element_type=jnp.float32
        )
    grad_queries = jnp.concatenate(query_parts, axis=0)
    return (
        grad_queries.astype(jnp.bfloat16),
        grad_keys.astype(jnp.bfloat16),
        grad_values.astype(jnp.bfloat16),
    )


def adam_update(weight, first, second, average, gradient, clip_scale, rate):
    clipped = clip_scale * gradient
    first_new = BETA_FIRST * first + (1.0 - BETA_FIRST) * clipped
    second_new = BETA_SECOND * second + (1.0 - BETA_SECOND) * clipped * clipped
    first_hat = first_new / (1.0 - BETA_FIRST**STEP)
    second_hat = second_new / (1.0 - BETA_SECOND**STEP)
    weight_new = weight - rate * (
        first_hat / (jnp.sqrt(second_hat) + ADAM_EPS) + WEIGHT_DECAY * weight
    )
    average_new = EMA_KEEP * average + (1.0 - EMA_KEEP) * weight_new
    return (weight_new, first_new, second_new, average_new)


def shards(
    x_rows,
    cotangent,
    task_ids,
    routes,
    norm_params,
    norm_first,
    norm_second,
    norm_ema,
    qkv_weight,
    qkv_first,
    qkv_second,
    qkv_ema,
    out_weight,
    out_first,
    out_second,
    out_ema,
    router,
    router_first,
    router_second,
    router_ema,
    expert_in,
    expert_in_first,
    expert_in_second,
    expert_in_ema,
    expert_out,
    expert_out_first,
    expert_out_second,
    expert_out_ema,
):
    qkv_full, out_full, in_full, eout_full = (
        lax.all_gather(qkv_weight.astype(jnp.bfloat16), "dp", axis=1, tiled=True),
        lax.all_gather(out_weight.astype(jnp.bfloat16), "dp", axis=0, tiled=True),
        lax.all_gather(expert_in.astype(jnp.bfloat16), "dp", axis=1, tiled=True),
        lax.all_gather(expert_out.astype(jnp.bfloat16), "dp", axis=1, tiled=True),
    )
    local_width = qkv_full.shape[2]
    local_heads = local_width // HD
    x_float = x_rows.astype(jnp.float32)
    first_normed, first_unit, first_inv = norm_forward(x_float, norm_params[0], norm_params[1])
    first_all = lax.all_gather(first_normed.astype(jnp.bfloat16), "mp", axis=0, tiled=True)
    triple = jnp.einsum(
        "rd,cdh->crh", first_all, qkv_full, preferred_element_type=jnp.float32
    ).astype(jnp.bfloat16)
    heads = triple.reshape(3, IMGS, L, local_heads, HD)
    context_heads, log_total = lax.map(
        lambda member: attend_image(member[0], member[1], member[2], QB),
        (heads[0], heads[1], heads[2]),
    )
    context = context_heads.reshape(R, local_width)
    attended_part = jnp.einsum("rh,dh->rd", context, out_full, preferred_element_type=jnp.float32)
    attended = lax.psum_scatter(
        attended_part.astype(jnp.bfloat16), "mp", scatter_dimension=0, tiled=True
    ).astype(jnp.float32)
    mid = x_float + attended
    second_normed, second_unit, second_inv = norm_forward(mid, norm_params[2], norm_params[3])
    second_all = lax.all_gather(second_normed.astype(jnp.bfloat16), "mp", axis=0, tiled=True)
    second_float = second_all.astype(jnp.float32)
    task_onehot = (task_ids[:, None] == jnp.arange(TASKS, dtype=jnp.int32)[None, :]).astype(
        jnp.float32
    )
    task_bias = dense_exact(task_onehot, router[D:])
    logits = dense_exact(second_float, router[:D])
    logits = (logits.reshape(IMGS, L, E) + task_bias[:, None, :]).reshape(R, E)
    route_hot = (routes[:, :, None] == jnp.arange(E, dtype=jnp.int32)[None, None, :]).astype(
        jnp.float32
    )
    chosen = jnp.sum(route_hot * logits[:, None, :], axis=-1)
    gates = jax.nn.softmax(chosen, axis=-1)
    slots = slot_table(routes, E, CAP)
    pair_ids = jnp.arange(R * TOP, dtype=jnp.int32)
    slot_pair = jnp.full((E * CAP,), R * TOP, jnp.int32).at[slots].set(pair_ids)
    slot_token = (slot_pair // TOP).reshape(E, CAP)
    gate_padded = jnp.concatenate([gates.reshape(-1), jnp.zeros((1,), jnp.float32)])
    slot_gate = gate_padded[slot_pair].reshape(E, CAP)
    padded_rows = jnp.concatenate([second_all, jnp.zeros((1, D), jnp.bfloat16)], axis=0)

    def expert_forward(carry, member):
        weight_in, weight_out, owners, owner_gate = member
        dispatched = padded_rows[owners]
        pre = jnp.dot(dispatched, weight_in, preferred_element_type=jnp.float32)
        hidden = gelu_exact(pre).astype(jnp.bfloat16)
        produced = jnp.einsum("cf,df->cd", hidden, weight_out, preferred_element_type=jnp.float32)
        return (carry.at[owners].add(owner_gate[:, None] * produced), None)

    mixture_acc, unused = lax.scan(
        expert_forward,
        jnp.zeros((R + 1, D), jnp.float32),
        (in_full, eout_full, slot_token, slot_gate),
    )
    mixture = lax.psum_scatter(
        mixture_acc[:R].astype(jnp.bfloat16), "mp", scatter_dimension=0, tiled=True
    ).astype(jnp.float32)
    output = mid + mixture
    grad_low_all = lax.all_gather(cotangent.astype(jnp.bfloat16), "mp", axis=0, tiled=True)
    grad_padded = jnp.concatenate([grad_low_all, jnp.zeros((1, D), jnp.bfloat16)], axis=0)

    def expert_backward(carry, member):
        weight_in, weight_out, owners, owner_gate = member
        dispatched = padded_rows[owners]
        pre = jnp.dot(dispatched, weight_in, preferred_element_type=jnp.float32)
        hidden = gelu_exact(pre).astype(jnp.bfloat16)
        produced = jnp.einsum("cf,df->cd", hidden, weight_out, preferred_element_type=jnp.float32)
        incoming = grad_padded[owners].astype(jnp.float32)
        slot_grad_gate = jnp.sum(incoming * produced, axis=-1)
        grad_produced = (owner_gate[:, None] * incoming).astype(jnp.bfloat16)
        grad_hidden = jnp.dot(grad_produced, weight_out, preferred_element_type=jnp.float32)
        grad_pre = (grad_hidden * gelu_slope(pre)).astype(jnp.bfloat16)
        grad_weight_out = jnp.einsum(
            "cd,cf->df", grad_produced, hidden, preferred_element_type=jnp.float32
        )
        grad_weight_in = jnp.einsum(
            "cd,cf->df", dispatched, grad_pre, preferred_element_type=jnp.float32
        )
        grad_dispatched = jnp.einsum(
            "cf,df->cd", grad_pre, weight_in, preferred_element_type=jnp.float32
        )
        return (
            carry.at[owners].add(grad_dispatched),
            (grad_weight_in, grad_weight_out, slot_grad_gate),
        )

    expert_carry, expert_outs = lax.scan(
        expert_backward,
        jnp.zeros((R + 1, D), jnp.float32),
        (in_full, eout_full, slot_token, slot_gate),
    )
    grad_in_stack, grad_eout_stack, slot_grad_gate = expert_outs
    in_reduced, eout_reduced = (
        lax.psum_scatter(grad_in_stack, "dp", scatter_dimension=1, tiled=True),
        lax.psum_scatter(grad_eout_stack, "dp", scatter_dimension=1, tiled=True),
    )
    grad_gates = slot_grad_gate.reshape(-1)[slots].reshape(R, TOP)
    grad_chosen = gates * (grad_gates - jnp.sum(gates * grad_gates, axis=-1, keepdims=True))
    grad_logits = jnp.sum(route_hot * grad_chosen[:, :, None], axis=1)
    router_rows_grad = dense_exact(second_float.T, grad_logits)
    task_rows_grad = dense_exact(task_onehot.T, jnp.sum(grad_logits.reshape(IMGS, L, E), axis=1))
    router_grad_part = jnp.concatenate([router_rows_grad, task_rows_grad], axis=0)
    grad_second_part = expert_carry[:R] + dense_exact(grad_logits, router[:D].T)
    grad_second = lax.psum_scatter(
        grad_second_part.astype(jnp.bfloat16), "mp", scatter_dimension=0, tiled=True
    ).astype(jnp.float32)
    grad_mid_norm, gain_two_grad, shift_two_grad = norm_backward(
        grad_second, second_unit, second_inv, norm_params[2]
    )
    grad_mid = cotangent + grad_mid_norm
    grad_mid_all = lax.all_gather(grad_mid.astype(jnp.bfloat16), "mp", axis=0, tiled=True)
    grad_out_weight = jnp.einsum(
        "rd,rh->dh", grad_mid_all, context, preferred_element_type=jnp.float32
    )
    grad_context = jnp.dot(grad_mid_all, out_full, preferred_element_type=jnp.float32).astype(
        jnp.bfloat16
    )
    grad_context_heads = grad_context.reshape(IMGS, L, local_heads, HD)
    grad_queries, grad_keys, grad_values = lax.map(
        lambda member: attend_image_back(member[0], member[1], member[2], member[3], member[4], QB),
        (heads[0], heads[1], heads[2], log_total, grad_context_heads),
    )
    grad_triple = jnp.stack(
        [
            grad_queries.reshape(R, local_width),
            grad_keys.reshape(R, local_width),
            grad_values.reshape(R, local_width),
        ],
        axis=0,
    )
    grad_qkv_weight = jnp.einsum(
        "rd,crh->cdh", first_all, grad_triple, preferred_element_type=jnp.float32
    )
    grad_first_part = jnp.einsum(
        "crh,cdh->rd", grad_triple, qkv_full, preferred_element_type=jnp.float32
    )
    grad_first = lax.psum_scatter(
        grad_first_part.astype(jnp.bfloat16), "mp", scatter_dimension=0, tiled=True
    ).astype(jnp.float32)
    grad_x_norm, gain_one_grad, shift_one_grad = norm_backward(
        grad_first, first_unit, first_inv, norm_params[0]
    )
    input_grad = grad_mid + grad_x_norm
    norm_grad_part = jnp.stack(
        [gain_one_grad, shift_one_grad, gain_two_grad, shift_two_grad], axis=0
    )
    norm_grad, router_grad = lax.psum((norm_grad_part, router_grad_part), ("dp", "mp"))
    qkv_reduced, out_reduced = (
        lax.psum_scatter(grad_qkv_weight, "dp", scatter_dimension=1, tiled=True),
        lax.psum_scatter(grad_out_weight, "dp", scatter_dimension=0, tiled=True),
    )
    local_squares = (
        jnp.sum(qkv_reduced * qkv_reduced)
        + jnp.sum(out_reduced * out_reduced)
        + jnp.sum(in_reduced * in_reduced)
        + jnp.sum(eout_reduced * eout_reduced)
    )
    share = 1.0 / (lax.axis_size("dp") * lax.axis_size("mp"))
    small_squares = jnp.sum(norm_grad * norm_grad) + jnp.sum(router_grad * router_grad)
    total_squares = lax.psum(local_squares + share * small_squares, ("dp", "mp"))
    grad_norm = jnp.sqrt(total_squares)
    clip_scale = jnp.minimum(1.0, CLIP_LIMIT / (grad_norm + 1e-06))
    norm_new, norm_first_new, norm_second_new, norm_ema_new = adam_update(
        norm_params, norm_first, norm_second, norm_ema, norm_grad, clip_scale, NORM_RATE
    )
    qkv_new, qkv_first_new, qkv_second_new, qkv_ema_new = adam_update(
        qkv_weight, qkv_first, qkv_second, qkv_ema, qkv_reduced, clip_scale, LEARN_RATE
    )
    out_new, out_first_new, out_second_new, out_ema_new = adam_update(
        out_weight, out_first, out_second, out_ema, out_reduced, clip_scale, LEARN_RATE
    )
    router_new, router_first_new, router_second_new, router_ema_new = adam_update(
        router, router_first, router_second, router_ema, router_grad, clip_scale, LEARN_RATE
    )
    in_new, in_first_new, in_second_new, in_ema_new = adam_update(
        expert_in,
        expert_in_first,
        expert_in_second,
        expert_in_ema,
        in_reduced,
        clip_scale,
        LEARN_RATE,
    )
    eout_new, eout_first_new, eout_second_new, eout_ema_new = adam_update(
        expert_out,
        expert_out_first,
        expert_out_second,
        expert_out_ema,
        eout_reduced,
        clip_scale,
        LEARN_RATE,
    )
    return (
        output,
        input_grad,
        grad_norm.reshape(1),
        norm_new,
        norm_first_new,
        norm_second_new,
        norm_ema_new,
        qkv_new,
        qkv_first_new,
        qkv_second_new,
        qkv_ema_new,
        out_new,
        out_first_new,
        out_second_new,
        out_ema_new,
        router_new,
        router_first_new,
        router_second_new,
        router_ema_new,
        in_new,
        in_first_new,
        in_second_new,
        in_ema_new,
        eout_new,
        eout_first_new,
        eout_second_new,
        eout_ema_new,
    )


def solution(mesh):
    return jax.shard_map(
        shards,
        mesh=mesh,
        in_specs=(
            P(("dp", "mp"), None),
            P(("dp", "mp"), None),
            P("dp"),
            P("dp", None),
            P(),
            P(),
            P(),
            P(),
            P(None, "dp", "mp"),
            P(None, "dp", "mp"),
            P(None, "dp", "mp"),
            P(None, "dp", "mp"),
            P("dp", "mp"),
            P("dp", "mp"),
            P("dp", "mp"),
            P("dp", "mp"),
            P(),
            P(),
            P(),
            P(),
            P(None, "dp", "mp"),
            P(None, "dp", "mp"),
            P(None, "dp", "mp"),
            P(None, "dp", "mp"),
            P(None, "dp", "mp"),
            P(None, "dp", "mp"),
            P(None, "dp", "mp"),
            P(None, "dp", "mp"),
        ),
        out_specs=(
            P(("dp", "mp"), None),
            P(("dp", "mp"), None),
            P(),
            P(),
            P(),
            P(),
            P(),
            P(None, "dp", "mp"),
            P(None, "dp", "mp"),
            P(None, "dp", "mp"),
            P(None, "dp", "mp"),
            P("dp", "mp"),
            P("dp", "mp"),
            P("dp", "mp"),
            P("dp", "mp"),
            P(),
            P(),
            P(),
            P(),
            P(None, "dp", "mp"),
            P(None, "dp", "mp"),
            P(None, "dp", "mp"),
            P(None, "dp", "mp"),
            P(None, "dp", "mp"),
            P(None, "dp", "mp"),
            P(None, "dp", "mp"),
            P(None, "dp", "mp"),
        ),
        check_vma=False,
    )
```

profile of v0, /device:TPU:0, one launch (start us, length us, event | category | flops | bytes accessed | tf_op | source)
XLA Modules:
  0.0 1747.6 jit_solution(17913996117398227735)
XLA Ops:
  13.7 43.5 %all_gather.26 = bf16[384,192]{1,0:T(8,128)(2,1)S(1)} all-gather(bf16[24,192]{1,0:T(8,128)(2,1)S(1)} %convert_element_type.177), channel_id=1, replica_groups=mesh['dp'=16,'mp'=2] {'dp'}, dimensions={0}, use_global_device_ids=true | all-gather | bytes 156672 | tf_op jit(solution)/shard_map/all_gather | solution.py:178
  57.3 38.6 %all_gather.25 = bf16[3,384,192]{2,1,0:T(8,128)(2,1)S(1)} all-gather(bf16[3,24,192]{2,1,0:T(8,128)(2,1)S(1)} %convert_element_type.165), channel_id=1, replica_groups=mesh['dp'=16,'mp'=2] {'dp'}, dimensions={1}, use_global_device_ids=true | all-gather | bytes 470016 | tf_op jit(solution)/shard_map/all_gather | solution.py:177
  122.4 5.8 reduce-scatter.8.cloned.1.call-done
  139.9 23.0 %scatter_custom_fusion.2 = s32[12288]{0:T(1024)S(1)} fusion(s32[6144]{0:T(1024)S(1)} %bitcast.231, s32[6144]{0:T(1024)S(1)} %iota.21, s32[]{:T(128)} %constant.100.clone.1), kind=kCustom, calls=%fused_computation.217 | custom fusion | bytes 49156 | tf_op jit(solution)/shard_map/scatter | solution.py:217
  169.6 68.5 %gather_fusion.3 = f32[12288]{0:T(1024)S(1)} fusion(f32[6145]{0:T(1024)S(1)} %pad_maximum_fusion.2, s32[12288]{0:T(1024)S(1)} %get-tuple-element.373), kind=kCustom, calls=%fused_computation.3 | custom fusion | bytes 147456 | tf_op jit(solution)/shard_map/gather | solution.py:220
  238.9 82.2 %all-gather.13.cloned.1.call-done = bf16[8,384,768]{2,1,0:T(8,128)(2,1)} async-done(((bf16[8,24,768]{2,1,0:T(8,128)(2,1)}), bf16[8,384,768]{2,1,0:T(8,128)(2,1)}) %all-gather.13.cloned.1.call-update) | async-done | bytes 4718608 | tf_op jit(solution)/shard_map/all_gather | solution.py:180
  322.7 408.2 %while.5 = (s32[]{:T(128)}, f32[1537,384]{1,0:T(8,128)}, f32[8,384,768]{2,1,0:T(8,128)}, f32[8,384,768]{2,1,0:T(8,128)}, f32[8,1536]{1,0:T(8,128)}, /*index=5*/s...) while((s32[]{:T(128)}, f32[1537,384]{1,0:T(8,128)}, ...), condition=%wide.region_25.26_spmd, body=%wide.region_22.25_spmd.sunk | while | flops 5459416064 | bytes 69727472 | solution.py:268
  324.2 4.8 gather_fusion.1
  333.7 5.4 gather_fusion.2
  355.3 14.4 scatter_fusion.1
  375.5 4.8 gather_fusion.1
  385.1 5.4 gather_fusion.2
  406.6 13.9 scatter_fusion.1
  426.3 4.8 gather_fusion.1
  435.8 5.4 gather_fusion.2
  457.4 14.4 scatter_fusion.1
  477.6 4.8 gather_fusion.1
  487.1 5.4 gather_fusion.2
  508.7 14.4 scatter_fusion.1
  528.9 4.8 gather_fusion.1
  538.4 5.4 gather_fusion.2
  560.0 14.7 scatter_fusion.1
  580.5 4.8 gather_fusion.1
  590.0 5.4 gather_fusion.2
  611.6 14.3 scatter_fusion.1
  631.7 4.8 gather_fusion.1
  641.2 5.4 gather_fusion.2
  662.8 13.3 scatter_fusion.1
  691.5 5.4 gather_fusion.2
  713.0 13.6 scatter_fusion.1
  731.8 34.7 %gather_fusion.4 = f32[6144]{0:T(1024)S(1)} fusion(f32[12288]{0:T(1024)S(1)} %reshape.416, s32[6144]{0:T(1024)} %broadcast_clamp_fusion), kind=kCustom, calls=%fused_computation.4 | custom fusion | bytes 73728 | tf_op jit(solution)/shard_map/gather | solution.py:278
  775.1 202.2 %while.4 = (s32[]{:T(128)}, f32[1537,384]{1,0:T(8,128)}, s32[8,1536]{1,0:T(8,128)}, f32[8,1536]{1,0:T(8,128)}, bf16[1537,384]{1,0:T(8,128)(2,1)S(1)}, /*index=5*...) while((s32[]{:T(128)}, f32[1537,384]{1,0:T(8,128)}, s32[8,1536]{1,0:T(8,128)}, ...), condition=%wide.region_20.21_spmd, body=%wide.region_18.20_spmd.sunk | while | flops 1819023872 | bytes 14216285 | solution.py:231
  776.0 5.3 gather_fusion
  786.9 13.7 scatter_fusion
  801.5 5.3 gather_fusion
  812.5 13.2 scatter_fusion
  826.5 5.3 gather_fusion
  837.5 13.7 scatter_fusion
  852.1 5.3 gather_fusion
  863.0 13.7 scatter_fusion
  877.6 5.3 gather_fusion
  888.5 14.0 scatter_fusion
  903.4 5.3 gather_fusion
  914.4 13.7 scatter_fusion
  928.9 5.3 gather_fusion
  939.8 12.7 scatter_fusion
  953.4 5.3 gather_fusion
  964.3 13.0 scatter_fusion
  982.8 4.9 reduce-scatter.10.cloned.1.call-done
  991.4 10.4 all-gather.17.cloned.1.call-done
  1003.7 8.4 multiply_reduce_fusion.1
  1012.2 5.6 fusion.46
  1017.8 5.1 multiply_reduce_fusion
  1022.9 6.3 multiply_convert_fusion.2
  1031.6 5.1 multiply_reduce_fusion.2
  1036.7 8.7 multiply_convert_fusion.4
  1049.6 7.6 multiply_convert_fusion.3
  1088.8 107.8 %reduce-scatter.16.cloned.1.call-done = f32[24,192]{1,0:T(8,128)} async-done(((f32[384,192]{1,0:T(8,128)}), f32[24,192]{1,0:T(8,128)}) %reduce-scatter.16.cloned.1.call-update) | async-done | bytes 18448 | tf_op jit(solution)/shard_map/reduce_scatter | solution.py:331
  1198.0 120.5 %all-reduce.6.cloned.1.call-done = f32[3,384,192]{2,0,1:T(4,128)} async-done(((f32[3,384,192]{2,0,1:T(4,128)}), f32[3,384,192]{2,0,1:T(4,128)}) %all-reduce.6.cloned.1.call-update) | async-done | bytes 884752
  1322.0 7.4 reduce-scatter.14.cloned.1.call-done
  1331.2 42.3 %all-reduce.3 = (f32[4,384]{1,0:T(4,128)S(1)}, f32[389,8]{0,1:T(8,128)S(1)}) all-reduce(f32[4,384]{1,0:T(4,128)S(1)} %pad_maximum_fusion.4, f32[389,8]{0,1:T(8,128)S(1)} %pad_maximum_fusion.3), channel_id=1, replica_groups=mesh['dp'=16,'mp'=2] {'dp','mp'}, use_global_device_ids=true, to_apply=%region_49.50 | all-reduce | flops 4648 | bytes 37184 | tf_op jit(solution)/shard_map/psum | solution.py:328
  1377.2 130.6 %reduce-scatter.18.cloned.1.call-done = f32[8,24,768]{2,1,0:T(8,128)} async-done(((f32[8,384,768]{2,1,0:T(8,128)}), f32[8,24,768]{2,1,0:T(8,128)}) %reduce-scatter.18.cloned.1.call-update) | async-done | bytes 589840 | tf_op jit(solution)/shard_map/reduce_scatter | solution.py:275
  1510.3 174.0 %reduce-scatter.20.cloned.1.call-done = f32[8,24,768]{2,1,0:T(8,128)} async-done(((f32[8,384,768]{2,1,0:T(8,128)}), f32[8,24,768]{2,1,0:T(8,128)}) %reduce-scatter.20.cloned.1.call-update) | async-done | bytes 589840 | tf_op jit(solution)/shard_map/reduce_scatter | solution.py:276
  1689.2 39.1 %psum.23 = f32[]{:T(128)} all-reduce(f32[]{:T(128)S(6)} %add.362), channel_id=1, replica_groups=mesh['dp'=16,'mp'=2] {'dp','mp'}, use_global_device_ids=true, to_apply=%region_54.55 | all-reduce | flops 1 | bytes 8 | tf_op jit(solution)/shard_map/psum | solution.py:341
  (551 shorter events, 403.0 us)
Async XLA Ops:
  7.2 6.5 copy-start.49
  7.2 6.5 copy-start.64
  7.2 88.6 %all-gather.7.cloned.1.call-start = ((), (), s32[]{:S(2)}) async-start(), calls=%async_computation.7 | async-start | bytes 1769472 | tf_op jit(solution)/shard_map/all_gather | solution.py:186
  10.8 120.2 %copy-start.86 = (f32[384]{0:T(512)}, f32[384]{0:T(512)S(1)}, u32[]{:S(2)}) copy-start(f32[384]{0:T(512)S(1)} %get-tuple-element.293) | copy-start | bytes 4612
  13.6 114.6 %reduce-scatter.8.cloned.1.call-start = ((), (), s32[]{:S(2)}) async-start(), calls=%async_computation.8 | async-start | bytes 1769472 | tf_op jit(solution)/shard_map/reduce_scatter | solution.py:197
  57.2 61.7 %copy-start.36 = (bf16[384,192]{1,0:T(8,128)(2,1)}, bf16[384,192]{1,0:T(8,128)(2,1)S(1)}, u32[]{:S(2)}) copy-start(bf16[384,192]{1,0:T(8,128)(2,1)S(1)} %all_gather.26) | copy-start | bytes 442372
  98.6 12.5 copy-start.8
  98.6 15.7 copy-start.16
  98.7 12.4 copy-start.29
  101.7 6.7 copy-start.2
  101.7 6.7 copy-start.69
  119.7 8.5 copy-start.4
  121.4 42.9 %all-gather.15.cloned.1.call-start = ((), (), s32[]{:S(2)}) async-start(), calls=%async_computation.13 | async-start | bytes 1769472 | tf_op jit(solution)/shard_map/all_gather | solution.py:240
  122.4 10.0 copy-start.24
  122.4 43.4 %all-gather.9.cloned.1.call-start = ((), (), s32[]{:S(2)}) async-start(), calls=%async_computation.9 | async-start | bytes 1769472 | tf_op jit(solution)/shard_map/all_gather | solution.py:202
  132.3 106.6 %all-gather.11.cloned.1.call-start = ((), (), s32[]{:S(2)}) async-start(), calls=%async_computation.10 | async-start | bytes 5013504 | tf_op jit(solution)/shard_map/all_gather | solution.py:179
  133.1 188.0 %all-gather.13.cloned.1.call-start = ((), (), s32[]{:S(2)}) async-start(), calls=%async_computation.11 | async-start | bytes 5013504 | tf_op jit(solution)/shard_map/all_gather | solution.py:180
  134.0 846.4 %reduce-scatter.12.cloned.1.call-start = ((), (), s32[]{:S(2)}) async-start(), calls=%async_computation.14 | async-start | bytes 1769472 | tf_op jit(solution)/shard_map/reduce_scatter | solution.py:285
  134.7 28.9 %copy-start.57 = (f32[389,8]{0,1:T(8,128)S(1)}, f32[389,8]{0,1:T(8,128)}, u32[]{:S(2)}) copy-start(f32[389,8]{0,1:T(8,128)} %param.48) | copy-start | bytes 37348
  168.9 69.3 %copy-start.55 = (f32[1536]{0:T(1024)}, f32[1536]{0:T(1024)S(1)}, u32[]{:S(2)}) copy-start(f32[1536]{0:T(1024)S(1)} %fusion.122) | copy-start | bytes 18436
  169.6 69.2 %copy-start.14 = (bf16[1536,384]{1,0:T(8,128)(2,1)S(1)}, bf16[1536,384]{1,0:T(8,128)(2,1)}, u32[]{:S(2)}) copy-start(bf16[1536,384]{1,0:T(8,128)(2,1)} %all-gather.9.cloned.1.call-done) | copy-start | bytes 3538948
  355.3 14.4 copy-start.11
  406.6 13.9 copy-start.11
  457.4 14.4 copy-start.11
  508.7 14.4 copy-start.11
  560.0 14.7 copy-start.11
  611.6 14.3 copy-start.11
  662.8 13.4 copy-start.11
  713.0 13.7 copy-start.11
  731.8 35.8 %copy-start.39 = (f32[1536,4]{0,1:T(4,128)S(1)}, f32[1536,4]{0,1:T(4,128)}, u32[]{:S(2)}) copy-start(f32[1536,4]{0,1:T(4,128)} %copy-done.38) | copy-start | bytes 73732
  731.8 35.8 %copy-start.51 = (f32[1536]{0:T(1024)S(1)}, f32[1536]{0:T(1024)}, u32[]{:S(2)}) copy-start(f32[1536]{0:T(1024)} %copy-done.50) | copy-start | bytes 18436
  731.8 35.8 %copy-start.56 = (f32[1536]{0:T(1024)S(1)}, f32[1536]{0:T(1024)}, u32[]{:S(2)}) copy-start(f32[1536]{0:T(1024)} %copy-done.55) | copy-start | bytes 18436
  731.8 35.9 %copy-start.48 = (s32[1536,4]{0,1:T(4,128)S(1)}, s32[1536,4]{0,1:T(4,128)}, u32[]{:S(2)}) copy-start(s32[1536,4]{0,1:T(4,128)} %param.35) | copy-start | bytes 73732
  731.8 37.2 %copy-start.58 = (f32[389,8]{0,1:T(8,128)S(1)}, f32[389,8]{0,1:T(8,128)}, u32[]{:S(2)}) copy-start(f32[389,8]{0,1:T(8,128)} %param.48) | copy-start | bytes 37348
  773.5 214.2 %reduce-scatter.10.cloned.1.call-start = ((), (), s32[]{:S(2)}) async-start(), calls=%async_computation.12 | async-start | bytes 1769472 | tf_op jit(solution)/shard_map/reduce_scatter | solution.py:236
  980.3 21.5 %all-gather.17.cloned.1.call-start = ((), (), s32[]{:S(2)}) async-start(), calls=%async_computation.15 | async-start | bytes 1769472 | tf_op jit(solution)/shard_map/all_gather | solution.py:292
  987.7 14.1 copy-start.37
  991.2 12.5 copy-start.17
  991.2 205.4 %reduce-scatter.16.cloned.1.call-start = ((), (), s32[]{:S(2)}) async-start(), calls=%async_computation.17 | async-start | bytes 417792 | tf_op jit(solution)/shard_map/reduce_scatter | solution.py:331
  1003.7 14.0 slice-start.3
  1003.7 14.0 slice-start.4
  1012.2 5.6 slice-start.5
  1022.9 8.6 slice-start
  1022.9 6.3 copy-start.9
  1022.9 8.6 slice-start.1
  1022.9 8.6 slice-start.2
  1036.6 13.0 slice-start.6
  1036.7 8.7 copy-start.32
  1036.7 13.0 slice-start.7
  1036.7 13.0 slice-start.8
  1074.0 4.8 copy-start.52
  1074.0 244.5 %all-reduce.6.cloned.1.call-start = ((), (), s32[]{:S(2)}) async-start(), calls=%async_computation.20 | async-start | bytes 3145728
  1081.5 247.8 %reduce-scatter.14.cloned.1.call-start = ((), (), s32[]{:S(2)}) async-start(), calls=%async_computation.16 | async-start | bytes 1769472 | tf_op jit(solution)/shard_map/reduce_scatter | solution.py:318
  1085.4 422.4 %reduce-scatter.18.cloned.1.call-start = ((), (), s32[]{:S(2)}) async-start(), calls=%async_computation.18 | async-start | bytes 10027008 | tf_op jit(solution)/shard_map/reduce_scatter | solution.py:275
  1086.2 598.2 %reduce-scatter.20.cloned.1.call-start = ((), (), s32[]{:S(2)}) async-start(), calls=%async_computation.19 | async-start | bytes 10027008 | tf_op jit(solution)/shard_map/reduce_scatter | solution.py:276
  1086.3 243.0 %copy-start.61 = (f32[768]{0:T(1024)S(1)}, f32[768]{0:T(1024)}, u32[]{:S(2)}) copy-start(f32[768]{0:T(1024)} %copy-done.60) | copy-start | bytes 9220
  1086.3 243.0 %copy-start.74 = (f32[768]{0:T(1024)S(1)}, f32[768]{0:T(1024)}, u32[]{:S(2)}) copy-start(f32[768]{0:T(1024)} %copy-done.73) | copy-start | bytes 9220
  1086.3 243.0 %copy-start.79 = (f32[384]{0:T(512)S(1)}, f32[384]{0:T(512)}, u32[]{:S(2)}) copy-start(f32[384]{0:T(512)} %copy-done.78) | copy-start | bytes 4612
  1329.3 357.6 %copy-start.28 = (bf16[768,384]{1,0:T(8,128)(2,1)S(1)}, bf16[768,384]{1,0:T(8,128)(2,1)}, u32[]{:S(2)}) copy-start(bf16[768,384]{1,0:T(8,128)(2,1)} %reduce-scatter.14.cloned.1.call-done) | copy-start | bytes 1769476
  1373.5 310.8 %copy-start.77 = (f32[389,8]{0,1:T(8,128)}, f32[389,8]{0,1:T(8,128)S(1)}, u32[]{:S(2)}) copy-start(f32[389,8]{0,1:T(8,128)S(1)} %get-tuple-element.333) | copy-start | bytes 37348
  1373.5 310.8 %copy-start.91 = (f32[4,384]{1,0:T(4,128)}, f32[4,384]{1,0:T(4,128)S(1)}, u32[]{:S(2)}) copy-start(f32[4,384]{1,0:T(4,128)S(1)} %get-tuple-element.332) | copy-start | bytes 18436
  1377.2 351.8 %copy-start.59 = (f32[389,8]{0,1:T(8,128)S(1)}, f32[389,8]{0,1:T(8,128)}, u32[]{:S(2)}) copy-start(f32[389,8]{0,1:T(8,128)} %param.48) | copy-start | bytes 37348
  1686.2 47.4 %copy-start.23 = (f32[8,24,768]{2,1,0:T(8,128)S(1)}, f32[8,24,768]{2,1,0:T(8,128)}, u32[]{:S(2)}) copy-start(f32[8,24,768]{2,1,0:T(8,128)} %param.56) | copy-start | bytes 1769476
  1686.2 47.4 %copy-start.27 = (f32[8,24,768]{2,1,0:T(8,128)S(1)}, f32[8,24,768]{2,1,0:T(8,128)}, u32[]{:S(2)}) copy-start(f32[8,24,768]{2,1,0:T(8,128)} %reduce-scatter.20.cloned.1.call-done) | copy-start | bytes 1769476
  (84 other events, 202.0 us)
Sparse Core Ops, SparseCore 0:
  13.7 11.9 all-gather.6
  121.5 6.6 reduce-scatter.7
  130.4 10.4 all-gather.14
  142.9 10.4 all-gather.8
  156.8 81.6 all-gather.10
  242.0 79.0 all-gather.12
  773.6 7.2 reduce-scatter.11
  980.4 7.2 reduce-scatter.9
  991.3 10.4 all-gather.16
  1074.1 122.4 reduce-scatter.15
  1202.0 116.4 all-reduce.5
  1321.3 7.9 reduce-scatter.13
  1335.0 172.8 reduce-scatter.17
  1514.3 169.9 reduce-scatter.19
where the time goes:
time: 1760 us; the launch traced here: 1750 us
  waiting for transfers between devices  645 us (37%)
  local copies, waits for them, and re-layouts  323 us (18%)
  other arithmetic  312 us (18%)
  matrix products  280 us (16%)
  blocking collectives  163 us (9%)
  between operations  23.1 us (1%)
    reduce_scatter x1, waiting for transfers between devices, shards(): lax.psum_scatter(grad_eout_stack, 'dp', scatter_dimension=1, tiled=True)  174 us
    reduce_scatter x1, waiting for transfers between devices, shards(): lax.psum_scatter(grad_in_stack, 'dp', scatter_dimension=1, tiled=True)  131 us
    unnamed x15, waiting for transfers between devices  122 us
    scatter-add x8, other arithmetic, expert_backward(): carry.at[owners].add(grad_dispatched)  113 us
    scatter-add x8, other arithmetic, expert_forward(): return (carry.at[owners].add(owner_gate[:, None] * produced), None)  108 us
    reduce_scatter x1, waiting for transfers between devices, shards(): lax.psum_scatter(grad_out_weight, 'dp', scatter_dimension=0, tiled=True)  108 us
    all_gather x1, waiting for transfers between devices, shards(): lax.all_gather(expert_out.astype(jnp.bfloat16), 'dp', axis=1, tiled=True)  82.2 us
    gather x1, local copies, waits for them, and re-layouts, shards(): slot_gate = gate_padded[slot_pair].reshape(E, CAP)  68.5 us
  transfers between devices with their start and end apart: 14, of which 9 were waited for; matrix products, arithmetic and copies ran while one was open for 19% of the time, Pallas kernels for 0%

commit v1 on v0

--- a/solution.py
+++ b/solution.py
@@ -1,6 +1,8 @@
 import jax
 import jax.numpy as jnp
 from jax import lax
+from jax.experimental import pallas as pl
+from jax.experimental.pallas import tpu as pltpu
 from jax.sharding import PartitionSpec as P
 
 D = 384
@@ -143,6 +145,809 @@
     return (weight_new, first_new, second_new, average_new)
 
 
+F32 = jnp.float32
+BF16 = jnp.bfloat16
+MESH = pl.DeviceIdType.MESH
+LOG2E = 1.4426950408889634
+NN = ((1,), (0,))
+NT = ((1,), (1,))
+TN = ((0,), (0,))
+GRID_Z, GRID_Y, GRID_X = 4, 2, 2
+ROW_BLOCK = 256
+
+
+def mm(left, right, dims=NN):
+    return lax.dot_general(left, right, (dims, ((), ())), preferred_element_type=F32)
+
+
+def row_stats(rows):
+    centered = rows - jnp.mean(rows, axis=-1, keepdims=True)
+    inv_std = lax.rsqrt(jnp.mean(centered * centered, axis=-1, keepdims=True) + NORM_EPS)
+    return centered * inv_std, inv_std
+
+
+def row_back(upstream, unit, inv_std, gain):
+    scaled = upstream * gain
+    inner = jnp.mean(scaled * unit, axis=-1, keepdims=True)
+    return inv_std * (scaled - jnp.mean(scaled, axis=-1, keepdims=True) - unit * inner)
+
+
+def step_kernel(
+    x_ref,
+    cot_ref,
+    task_ref,
+    routes_ref,
+    norm_ref,
+    qkv_ref,
+    wo_ref,
+    router_ref,
+    win_ref,
+    wout_ref,
+    out_ref,
+    igrad_ref,
+    red_ref,
+    redq_ref,
+    small_ref,
+    sumsq_ref,
+    p_hbm,
+    x_sib,
+    g_all,
+    x1,
+    qs,
+    ks,
+    vs,
+    ctx,
+    att_s,
+    att_r,
+    mid,
+    x2,
+    gates,
+    wgt,
+    mix,
+    gsec,
+    gs_r,
+    mix_s,
+    mix_r,
+    gm_own,
+    gml,
+    gctx,
+    gfirst_s,
+    gfirst_r,
+    gw,
+    r1,
+    r2,
+    r3,
+    gq,
+    gg,
+    q1,
+    q2,
+    q3,
+    ar_s,
+    ar_r,
+    sc_s,
+    sc_r,
+    ag_ss,
+    ag_rs,
+    rs_ss,
+    rs_rs,
+    gq_ss,
+    gq_rs,
+    gr_ss,
+    gr_rs,
+    sib_ss,
+    sib_rs,
+    att_ss,
+    att_rs,
+    gs_ss,
+    gs_rs,
+    ar_ss,
+    ar_rs,
+    sc_ss,
+    sc_rs,
+    p_sem,
+):
+    experts = win_ref.shape[0]
+    half = x_ref.shape[0]
+    rows_all = 2 * half
+    width = qs.shape[1]
+    heads = width // HD
+    tb = ROW_BLOCK
+    blocks = rows_all // tb
+    own_blocks = half // tb
+
+    d = lax.axis_index("dp")
+    m = lax.axis_index("mp")
+    z = d // 4
+    y = (d // 2) % 2
+    x = d % 2
+    sib = (d, 1 - m)
+    xn = (d + 1 - 2 * x, m)
+    yn = (d + 2 - 4 * y, m)
+    zs = [((z + k) % 4) for k in (1, 2, 3)]
+    zn = [(zs[k] * 4 + y * 2 + x, m) for k in range(3)]
+
+    barrier = pltpu.get_barrier_semaphore()
+    for peer in [sib, xn, yn] + zn:
+        pl.semaphore_signal(barrier, inc=1, device_id=peer, device_id_type=MESH)
+    pl.semaphore_wait(barrier, 6)
+
+    def rcopy(src, dst, ss, rs, dev):
+        return pltpu.make_async_remote_copy(
+            src_ref=src, dst_ref=dst, send_sem=ss, recv_sem=rs, device_id=dev, device_id_type=MESH
+        )
+
+    def own_rows(b):
+        return pl.ds(pl.multiple_of(m * half + b * tb, tb), tb)
+
+    def sib_rows(b):
+        return pl.ds(pl.multiple_of((1 - m) * half + b * tb, tb), tb)
+
+    def blk_rows(b):
+        return pl.ds(pl.multiple_of(b * tb, tb), tb)
+
+    own_half = pl.ds(pl.multiple_of(m * half, half), half)
+
+    def ag1(e):
+        return [
+            rcopy(gw.at[:, e, z, y, x], gw.at[:, e, z, y, x], ag_ss.at[e, k], ag_rs.at[e, k], zn[k])
+            for k in range(3)
+        ]
+
+    def ag2(e):
+        return [
+            rcopy(gw.at[0, e, :, y, x], gw.at[0, e, :, y, x], ag_ss.at[e, 3], ag_rs.at[e, 3], xn),
+            rcopy(gw.at[1, e, :, y, x], gw.at[1, e, :, y, x], ag_ss.at[e, 4], ag_rs.at[e, 4], yn),
+        ]
+
+    def ag3(e):
+        return [
+            rcopy(gw.at[0, e, :, y], gw.at[0, e, :, y], ag_ss.at[e, 5], ag_rs.at[e, 5], yn),
+            rcopy(gw.at[1, e, :, :, x], gw.at[1, e, :, :, x], ag_ss.at[e, 6], ag_rs.at[e, 6], xn),
+        ]
+
+    def start(copies):
+        for c in copies:
+            c.start()
+
+    def arrive(copies):
+        for c in copies:
+            c.wait_recv()
+
+    def sent(copies):
+        for c in copies:
+            c.wait_send()
+
+    def ag_tick(t):
+        @pl.when(jnp.logical_and(t >= 0, t < experts))
+        def _():
+            arrive(ag1(t))
+            start(ag2(t))
+
+        @pl.when(t + 2 < experts)
+        def _():
+            start(ag1(t + 2))
+
+        @pl.when(jnp.logical_and(t >= 1, t < experts + 1))
+        def _():
+            arrive(ag2(t - 1))
+            start(ag3(t - 1))
+
+        @pl.when(jnp.logical_and(t >= 2, t < experts + 2))
+        def _():
+            arrive(ag3(t - 2))
+
+    def rs1(e):
+        return [
+            rcopy(gw.at[0, e, :, 1 - y], r1.at[e, 0], rs_ss.at[e, 0], rs_rs.at[e, 0], yn),
+            rcopy(gw.at[1, e, :, :, 1 - x], r1.at[e, 1], rs_ss.at[e, 1], rs_rs.at[e, 1], xn),
+        ]
+
+    def rs2(e):
+        return [
+            rcopy(gw.at[0, e, :, y, 1 - x], r2.at[e, 0], rs_ss.at[e, 2], rs_rs.at[e, 2], xn),
+            rcopy(gw.at[1, e, :, 1 - y, x], r2.at[e, 1], rs_ss.at[e, 3], rs_rs.at[e, 3], yn),
+        ]
+
+    def rs3(e):
+        return [
+            rcopy(
+                gw.at[:, e, zs[k], y, x], r3.at[e, k], rs_ss.at[e, 4 + k], rs_rs.at[e, 4 + k], zn[k]
+            )
+            for k in range(3)
+        ]
+
+    def rs_tick(t):
+        @pl.when(jnp.logical_and(t >= 0, t < experts))
+        def _():
+            start(rs1(t))
+
+        @pl.when(jnp.logical_and(t >= 1, t < experts + 1))
+        def _():
+            e = t - 1
+            arrive(rs1(e))
+            gw[0, e, :, y] = (gw[0, e, :, y].astype(F32) + r1[e, 0].astype(F32)).astype(BF16)
+            gw[1, e, :, :, x] = (gw[1, e, :, :, x].astype(F32) + r1[e, 1].astype(F32)).astype(BF16)
+            start(rs2(e))
+
+        @pl.when(jnp.logical_and(t >= 2, t < experts + 2))
+        def _():
+            e = t - 2
+            arrive(rs2(e))
+            for a in range(2):
+                gw[a, e, :, y, x] = (
+                    gw[a, e, :, y, x].astype(F32) + r2[e, a].astype(F32)
+                ).astype(BF16)
+            start(rs3(e))
+
+        @pl.when(jnp.logical_and(t >= 3, t < experts + 3))
+        def _():
+            e = t - 3
+            arrive(rs3(e))
+            total = gw[:, e, z, y, x].astype(F32)
+            for k in range(3):
+                total = total + r3[e, k].astype(F32)
+            red_ref[:, e] = total
+
+    gq1 = [
+        rcopy(gq.at[:, z, y, x], gq.at[:, z, y, x], gq_ss.at[k], gq_rs.at[k], zn[k])
+        for k in range(3)
+    ]
+    gq2 = [
+        rcopy(gq.at[0:2, :, y, x], gq.at[0:2, :, y, x], gq_ss.at[3], gq_rs.at[3], xn),
+        rcopy(gq.at[2:4, :, y, x], gq.at[2:4, :, y, x], gq_ss.at[4], gq_rs.at[4], yn),
+    ]
+    gq3 = [
+        rcopy(gq.at[0:2, :, y], gq.at[0:2, :, y], gq_ss.at[5], gq_rs.at[5], yn),
+        rcopy(gq.at[2:4, :, :, x], gq.at[2:4, :, :, x], gq_ss.at[6], gq_rs.at[6], xn),
+    ]
+    gr1 = [
+        rcopy(gg.at[0:2, :, 1 - y], q1.at[0], gr_ss.at[0], gr_rs.at[0], yn),
+        rcopy(gg.at[2:4, :, :, 1 - x], q1.at[1], gr_ss.at[1], gr_rs.at[1], xn),
+    ]
+    gr2 = [
+        rcopy(gg.at[0:2, :, y, 1 - x], q2.at[0], gr_ss.at[2], gr_rs.at[2], xn),
+        rcopy(gg.at[2:4, :, 1 - y, x], q2.at[1], gr_ss.at[3], gr_rs.at[3], yn),
+    ]
+    gr3 = [
+        rcopy(gg.at[:, zs[k], y, x], q3.at[k], gr_ss.at[4 + k], gr_rs.at[4 + k], zn[k])
+        for k in range(3)
+    ]
+
+    send_x = rcopy(x_ref, x_sib, sib_ss.at[0], sib_rs.at[0], sib)
+    send_x.start()
+    for c in range(3):
+        gq[c, z, y, x] = qkv_ref[c].astype(BF16)
+    gq[3, z, y, x] = wo_ref[...].astype(BF16)
+    start(gq1)
+
+    def cast_weights(e, carry):
+        gw[0, e, z, y, x] = win_ref[e].astype(BF16)
+        gw[1, e, z, y, x] = wout_ref[e].astype(BF16)
+        return carry
+
+    lax.fori_loop(0, 2, cast_weights, 0)
+    start(ag1(0))
+    start(ag1(1))
+    lax.fori_loop(2, experts, cast_weights, 0)
+
+    def cast_cot(b, carry):
+        g_all[own_rows(b), :] = cot_ref[blk_rows(b), :].astype(BF16)
+        return carry
+
+    lax.fori_loop(0, own_blocks, cast_cot, 0)
+    send_g = rcopy(g_all.at[own_half], g_all.at[own_half], sib_ss.at[1], sib_rs.at[1], sib)
+    send_g.start()
+
+    gain1 = norm_ref[0:1, :]
+    bias1 = norm_ref[1:2, :]
+    gain2 = norm_ref[2:3, :]
+    bias2 = norm_ref[3:4, :]
+
+    def first_norm(rows, source, b):
+        unit, _ = row_stats(source[blk_rows(b), :].astype(F32))
+        x1[rows, :] = (unit * gain1 + bias1).astype(BF16)
+
+    def first_own(b, carry):
+        first_norm(own_rows(b), x_ref, b)
+        return carry
+
+    def first_sib(b, carry):
+        first_norm(sib_rows(b), x_sib, b)
+        return carry
+
+    lax.fori_loop(0, own_blocks, first_own, 0)
+    arrive(gq1)
+    start(gq2)
+    send_x.wait_recv()
+    lax.fori_loop(0, own_blocks, first_sib, 0)
+    arrive(gq2)
+    start(gq3)
+    ag_tick(jnp.int32(0))
+    arrive(gq3)
+
+    def flat(c):
+        return gq[c].reshape(D, width)
+
+    def project(b, carry):
+        r = blk_rows(b)
+        normed = x1[r, :]
+        qs[r, :] = (mm(normed, flat(0)).astype(BF16).astype(F32) * SCORE_SCALE).astype(BF16)
+        ks[r, :] = mm(normed, flat(1)).astype(BF16)
+        vs[r, :] = mm(normed, flat(2)).astype(BF16)
+        return carry
+
+    lax.fori_loop(0, blocks, project, 0)
+
+    def att_copy(b):
+        r = blk_rows(b)
+        return rcopy(att_s.at[r], att_r.at[r], att_ss.at[b], att_rs.at[b], sib)
+
+    def attention(pbuf):
+        def p_out(b):
+            return pltpu.make_async_copy(pbuf.at[b % 2], p_hbm.at[b], p_sem.at[b % 2])
+
+        def attend(b, carry):
+            r = blk_rows(b)
+
+            @pl.when(b >= 2)
+            def _():
+                p_out(b - 2).wait()
+
+            outs = []
+            for h in range(heads):
+                cs = slice(h * HD, (h + 1) * HD)
+                s = mm(qs[r, cs], ks[:, cs], NT)
+                powers = jnp.exp2((s - jnp.max(s, axis=1, keepdims=True)) * LOG2E)
+                inv = 1.0 / jnp.sum(powers, axis=1, keepdims=True)
+                prob = (powers * inv).astype(BF16)
+                pbuf[b % 2, h] = prob
+                outs.append(mm(prob, vs[:, cs]))
+            p_out(b).start()
+            context = jnp.concatenate(outs, axis=1).astype(BF16)
+            ctx[r, :] = context
+            att_s[r, :] = mm(context, flat(3), NT).astype(BF16)
+            att_copy(b).start()
+
+            @pl.when(b == 1)
+            def _():
+                ag_tick(jnp.int32(1))
+
+            @pl.when(b == 4)
+            def _():
+                ag_tick(jnp.int32(2))
+
+            return carry
+
+        lax.fori_loop(0, blocks, attend, 0)
+        p_out(blocks - 2).wait()
+        p_out(blocks - 1).wait()
+
+
+    pshape = (2, heads, tb, rows_all)
+    pl.run_scoped(attention, pltpu.VMEM(pshape, BF16))
+
+    router_main = router_ref[0:D, :]
+    router_hi = router_main.astype(BF16)
+    router_lo = (router_main - router_hi.astype(F32)).astype(BF16)
+    task = task_ref[0]
+    n_tasks = router_ref.shape[0] - D
+    task_pick = lax.broadcasted_iota(jnp.int32, (n_tasks, experts), 0) == task
+    task_bias = jnp.sum(jnp.where(task_pick, router_ref[D:, :], 0.0), axis=0, keepdims=True)
+    lane = lax.broadcasted_iota(jnp.int32, (tb, experts), 1)
+
+    def second_norm(rows, source, b, gb):
+        att_copy(gb).wait_recv()
+        rows_mid = (
+            source[blk_rows(b), :].astype(F32)
+            + att_s[rows, :].astype(F32)
+            + att_r[rows, :].astype(F32)
+        )
+        mid[rows, :] = rows_mid
+        unit, _ = row_stats(rows_mid)
+        normed = (unit * gain2 + bias2).astype(BF16)
+        x2[rows, :] = normed
+        logits = mm(normed, router_hi) + mm(normed, router_lo) + task_bias
+        picks = routes_ref[rows, :]
+        chosen = lane == picks[:, 0:1]
+        for k in range(1, TOP):
+            chosen = jnp.logical_or(chosen, lane == picks[:, k : k + 1])
+        peak = jnp.max(jnp.where(chosen, logits, -jnp.inf), axis=1, keepdims=True)
+        powers = jnp.where(chosen, jnp.exp(logits - peak), 0.0)
+        gates[rows, :] = powers / jnp.sum(powers, axis=1, keepdims=True)
+
+    def second_own(b, carry):
+        second_norm(own_rows(b), x_ref, b, m * own_blocks + b)
+        return carry
+
+    def second_sib(b, carry):
+        second_norm(sib_rows(b), x_sib, b, (1 - m) * own_blocks + b)
+        return carry
+
+    lax.fori_loop(0, own_blocks, second_own, 0)
+    lax.fori_loop(0, own_blocks, second_sib, 0)
+    send_g.wait_recv()
+    ag_tick(jnp.int32(3))
+
+    def clear(b, carry):
+        r = blk_rows(b)
+        mix[r, :] = jnp.zeros((tb, D), F32)
+        gsec[r, :] = jnp.zeros((tb, D), F32)
+        wgt[r, :] = jnp.zeros((tb, experts), F32)
+        return carry
+
+    lax.fori_loop(0, blocks, clear, 0)
+
+    def all_experts(g_gate, hid, gpre):
+        def expert(e, carry):
+            ag_tick(e + 4)
+            rs_tick(e - 1)
+
+            def block(b, carry2):
+                r = blk_rows(b)
+                w_in = gw[0, e].reshape(D, gw.shape[-1])
+                w_out = gw[1, e].reshape(D, gw.shape[-1])
+                gate = jnp.sum(jnp.where(lane == e, gates[r, :], 0.0), axis=1, keepdims=True)
+                pre = mm(x2[r, :], w_in)
+                incoming = (gate * g_all[r, :].astype(F32)).astype(BF16)
+                g_gate[r, :] = incoming
+                grad_hidden = mm(incoming, w_out)
+                phi = 0.5 + 0.5 * lax.erf(pre * SQRT_HALF)
+                density = jnp.exp2(pre * pre * (-0.5 * LOG2E)) * INV_SQRT_TWO_PI
+                hidden = (pre * phi).astype(BF16)
+                hid[r, :] = hidden
+                grad_pre = (grad_hidden * (phi + pre * density)).astype(BF16)
+                gpre[r, :] = grad_pre
+                produced = mm(hidden, w_out, NT)
+                mix[r, :] += gate * produced
+                weight = jnp.sum(incoming.astype(F32) * produced, axis=1, keepdims=True)
+                wgt[r, :] = jnp.where(lane == e, weight, wgt[r, :])
+                gsec[r, :] += mm(grad_pre, w_in, NT)
+                return carry2
+
+            lax.fori_loop(0, blocks, block, 0)
+            sent(ag1(e) + ag2(e) + ag3(e))
+            shape = gw.shape[2:]
+            gw[0, e] = mm(x2[...], gpre[...], TN).reshape(shape).astype(BF16)
+            gw[1, e] = mm(g_gate[...], hid[...], TN).reshape(shape).astype(BF16)
+            return carry
+
+        lax.fori_loop(0, experts, expert, 0)
+
+    pl.run_scoped(
+        all_experts,
+        pltpu.VMEM((rows_all, D), BF16),
+        pltpu.VMEM((rows_all, gw.shape[-1]), BF16),
+        pltpu.VMEM((rows_all, gw.shape[-1]), BF16),
+    )
+    rs_tick(jnp.int32(experts - 1))
+
+    def gs_copy(b):
+        r = blk_rows(b)
+        return rcopy(att_s.at[r], gs_r.at[r], gs_ss.at[b], gs_rs.at[b], sib)
+
+    for b in range(blocks):
+        att_copy(b).wait_send()
+
+    ones = jnp.ones((tb, 128), BF16)
+
+    def gate_grad(b, carry):
+        rg, tg = carry
+        r = blk_rows(b)
+        share = wgt[r, :]
+        grad_logits = share - gates[r, :] * jnp.sum(share, axis=1, keepdims=True)
+        high = grad_logits.astype(BF16)
+        low = (grad_logits - high.astype(F32)).astype(BF16)
+        att_s[r, :] = (gsec[r, :] + mm(high, router_hi, NT)).astype(BF16)
+        gs_copy(b).start()
+        normed = x2[r, :]
+        rg = rg + mm(high, normed, TN) + mm(low, normed, TN)
+        tg = tg + mm(high, ones, TN) + mm(low, ones, TN)
+        return rg, tg
+
+    rg, tg = lax.fori_loop(
+        0,
+        blocks,
+        gate_grad,
+        (jnp.zeros((experts, D), F32), jnp.zeros((experts, 128), F32)),
+    )
+    task_lane = lax.broadcasted_iota(jnp.int32, (experts, 128), 1) == task
+    ar_s[0] = jnp.zeros(ar_s.shape[1:], F32)
+    ar_s[0, 8:16, :] = rg
+    ar_s[0, 16:24, 0:128] = jnp.where(task_lane, tg, 0.0)
+
+    def mix_out(b, carry):
+        mix_s[blk_rows(b), :] = mix[sib_rows(b), :].astype(BF16)
+        return carry
+
+    lax.fori_loop(0, own_blocks, mix_out, 0)
+    send_mix = rcopy(mix_s, mix_r, sib_ss.at[2], sib_rs.at[2], sib)
+    send_mix.start()
+
+    def back_second(rows, gb):
+        gs_copy(gb).wait_recv()
+        grad_second = att_s[rows, :].astype(F32) + gs_r[rows, :].astype(F32)
+        unit, inv_std = row_stats(mid[rows, :])
+        back = row_back(grad_second, unit, inv_std, gain2)
+        return grad_second, unit, back
+
+    w_o = flat(3)
+
+    def back_own(b, carry):
+        gain_sum, bias_sum = carry
+        rows = own_rows(b)
+        grad_second, unit, back = back_second(rows, m * own_blocks + b)
+        grad_mid = cot_ref[blk_rows(b), :] + back
+        gm_own[blk_rows(b), :] = grad_mid
+        grad_low = grad_mid.astype(BF16)
+        gml[rows, :] = grad_low
+        gctx[rows, :] = mm(grad_low, w_o).astype(BF16)
+        gain_sum = gain_sum + jnp.sum(grad_second * unit, axis=0, keepdims=True)
+        bias_sum = bias_sum + jnp.sum(grad_second, axis=0, keepdims=True)
+        return gain_sum, bias_sum
+
+    def back_sib(b, carry):
+        rows = sib_rows(b)
+        grad_second, unit, back = back_second(rows, (1 - m) * own_blocks + b)
+        grad_low = (g_all[rows, :].astype(F32) + back).astype(BF16)
+        gml[rows, :] = grad_low
+        gctx[rows, :] = mm(grad_low, w_o).astype(BF16)
+        return carry
+
+    zero_row = jnp.zeros((1, D), F32)
+    gain2_grad, bias2_grad = lax.fori_loop(0, own_blocks, back_own, (zero_row, zero_row))
+    ar_s[0, 2:3, :] = gain2_grad
+    ar_s[0, 3:4, :] = bias2_grad
+    lax.fori_loop(0, own_blocks, back_sib, 0)
+    qshape = gg.shape[1:]
+    gg[3] = mm(gml[...], ctx[...], TN).reshape(qshape).astype(BF16)
+
+    def last_part(pbuf, keys_acc, values_acc, dq):
+        def p_in(b):
+            return pltpu.make_async_copy(p_hbm.at[b], pbuf.at[b % 2], p_sem.at[b % 2])
+
+        p_in(0).start()
+        keys_acc[...] = jnp.zeros(keys_acc.shape, F32)
+        values_acc[...] = jnp.zeros(values_acc.shape, F32)
+
+        def attend_back(b, carry):
+            r = blk_rows(b)
+
+            @pl.when(b + 1 < blocks)
+            def _():
+                p_in(b + 1).start()
+
+            p_in(b).wait()
+            outs = []
+            for h in range(heads):
+                cs = slice(h * HD, (h + 1) * HD)
+                grad_block = gctx[r, cs]
+                inner = jnp.sum(
+                    grad_block.astype(F32) * ctx[r, cs].astype(F32), axis=1, keepdims=True
+                )
+                grad_prob = mm(grad_block, vs[:, cs], NT)
+                prob = pbuf[b % 2, h]
+                grad_scores = (prob.astype(F32) * (grad_prob - inner)).astype(BF16)
+                outs.append(mm(grad_scores, ks[:, cs]) * SCORE_SCALE)
+                keys_acc[cs, :] += mm(qs[r, cs], grad_scores, TN)
+                values_acc[cs, :] += mm(grad_block, prob, TN)
+            dq[r, :] = jnp.concatenate(outs, axis=1).astype(BF16)
+            rs_tick(b + experts)
+            return carry
+
+        lax.fori_loop(0, blocks, attend_back, 0)
+
+        send_mix.wait_recv()
+
+        def write_out(b, carry):
+            r = blk_rows(b)
+            rows = own_rows(b)
+            out_ref[r, :] = mid[rows, :] + mix[rows, :] + mix_r[r, :].astype(F32)
+            return carry
+
+        lax.fori_loop(0, own_blocks, write_out, 0)
+
+        normed = x1[...]
+        gg[0] = mm(normed, dq[...], TN).reshape(qshape).astype(BF16)
+        gg[1] = mm(normed, keys_acc[...].astype(BF16), ((0,), (1,))).reshape(qshape).astype(BF16)
+        gg[2] = mm(normed, values_acc[...].astype(BF16), ((0,), (1,))).reshape(qshape).astype(BF16)
+        start(gr1)
+
+        def grad_first(rows):
+            return (
+                mm(dq[rows, :], flat(0), NT)
+                + mm(keys_acc[:, rows].astype(BF16), flat(1), ((0,), (1,)))
+                + mm(values_acc[:, rows].astype(BF16), flat(2), ((0,), (1,)))
+            )
+
+        def first_back_sib(b, carry):
+            gfirst_s[blk_rows(b), :] = grad_first(sib_rows(b)).astype(BF16)
+            return carry
+
+        def first_back_own(b, carry):
+            mix[blk_rows(b), :] = grad_first(own_rows(b))
+            return carry
+
+        lax.fori_loop(0, own_blocks, first_back_sib, 0)
+        send_first.start()
+        lax.fori_loop(0, own_blocks, first_back_own, 0)
+
+    send_first = rcopy(gfirst_s, gfirst_r, sib_ss.at[3], sib_rs.at[3], sib)
+    pl.run_scoped(
+        last_part,
+        pltpu.VMEM(pshape, BF16),
+        pltpu.VMEM((width, rows_all), F32),
+        pltpu.VMEM((width, rows_all), F32),
+        pltpu.VMEM((rows_all, width), BF16),
+    )
+
+    arrive(gr1)
+    gg[0:2, :, y] = (gg[0:2, :, y].astype(F32) + q1[0].astype(F32)).astype(BF16)
+    gg[2:4, :, :, x] = (gg[2:4, :, :, x].astype(F32) + q1[1].astype(F32)).astype(BF16)
+    start(gr2)
+
+    send_first.wait_recv()
+
+    def back_first(b, carry):
+        gain_sum, bias_sum = carry
+        r = blk_rows(b)
+        upstream = mix[r, :] + gfirst_r[r, :].astype(F32)
+        unit, inv_std = row_stats(x_ref[r, :].astype(F32))
+        igrad_ref[r, :] = gm_own[r, :] + row_back(upstream, unit, inv_std, gain1)
+        gain_sum = gain_sum + jnp.sum(upstream * unit, axis=0, keepdims=True)
+        bias_sum = bias_sum + jnp.sum(upstream, axis=0, keepdims=True)
+        return gain_sum, bias_sum
+
+    gain1_grad, bias1_grad = lax.fori_loop(0, own_blocks, back_first, (zero_row, zero_row))
+    ar_s[0, 0:1, :] = gain1_grad
+    ar_s[0, 1:2, :] = bias1_grad
+
+    arrive(gr2)
+    gg[0:2, :, y, x] = (gg[0:2, :, y, x].astype(F32) + q2[0].astype(F32)).astype(BF16)
+    gg[2:4, :, y, x] = (gg[2:4, :, y, x].astype(F32) + q2[1].astype(F32)).astype(BF16)
+    start(gr3)
+
+    def sum_all(src, dst, ss, rs):
+        for i, peer in enumerate([sib, xn, yn]):
+            c = rcopy(src.at[i], dst.at[i], ss.at[i], rs.at[i], peer)
+            c.start()
+            c.wait()
+            src[i + 1] = src[i] + dst[i]
+        dst[3 + z] = src[3]
+        copies = [
+            rcopy(src.at[3], dst.at[3 + z], ss.at[3 + k], rs.at[3 + k], zn[k]) for k in range(3)
+        ]
+        start(copies)
+        for c in copies:
+            c.wait()
+        return dst[3] + dst[4] + dst[5] + dst[6]
+
+    small = sum_all(ar_s, ar_r, ar_ss, ar_rs)
+    small_ref[...] = small
+
+    arrive(gr3)
+    total = gg[:, z, y, x].astype(F32)
+    for k in range(3):
+        total = total + q3[k].astype(F32)
+    redq_ref[...] = total
+
+    def squares(e, acc):
+        for a in range(2):
+            acc = acc + jnp.sum(red_ref[a, e] * red_ref[a, e])
+        return acc
+
+    share = 1.0 / (2 * GRID_Z * GRID_Y * GRID_X)
+    local_sum = lax.fori_loop(0, experts, squares, jnp.sum(total * total))
+    local_sum = local_sum + share * jnp.sum(small * small)
+    sc_s[0] = jnp.full(sc_s.shape[1:], local_sum, F32)
+    sumsq_ref[...] = sum_all(sc_s, sc_r, sc_ss, sc_rs)
+
+    sent(gq1 + gq2 + gq3 + gr1 + gr2 + gr3)
+
+    def drain(e, carry):
+        sent(rs1(e) + rs2(e) + rs3(e))
+        return carry
+
+    lax.fori_loop(0, experts, drain, 0)
+    for c in [send_x, send_g, send_mix, send_first]:
+        c.wait_send()
+
+    def drain_rows(b, carry):
+        gs_copy(b).wait_send()
+        return carry
+
+    lax.fori_loop(0, blocks, drain_rows, 0)
+
+
+def step_call(x_rows, cotangent, task_ids, routes, norms, qkv, wo, router, win, wout):
+    half = x_rows.shape[0]
+    rows_all = 2 * half
+    experts, shard, hidden = win.shape
+    width = wo.shape[1]
+    blocks = rows_all // ROW_BLOCK
+    heads = width // HD
+    vmem = pl.BlockSpec(memory_space=pltpu.VMEM)
+    grid = (GRID_Z, GRID_Y, GRID_X)
+    struct = jax.ShapeDtypeStruct
+    dma = pltpu.SemaphoreType.DMA
+    outs = (
+        struct((half, D), F32),
+        struct((half, D), F32),
+        struct((2, experts, shard, hidden), F32),
+        struct((4, shard, width), F32),
+        struct((24, D), F32),
+        struct((8, 128), F32),
+        struct((blocks, heads, ROW_BLOCK, rows_all), BF16),
+    )
+    scratch = [
+        pltpu.VMEM((half, D), BF16),
+        pltpu.VMEM((rows_all, D), BF16),
+        pltpu.VMEM((rows_all, D), BF16),
+        pltpu.VMEM((rows_all, width), BF16),
+        pltpu.VMEM((rows_all, width), BF16),
+        pltpu.VMEM((rows_all, width), BF16),
+        pltpu.VMEM((rows_all, width), BF16),
+        pltpu.VMEM((rows_all, D), BF16),
+        pltpu.VMEM((rows_all, D), BF16),
+        pltpu.VMEM((rows_all, D), F32),
+        pltpu.VMEM((rows_all, D), BF16),
+        pltpu.VMEM((rows_all, experts), F32),
+        pltpu.VMEM((rows_all, experts), F32),
+        pltpu.VMEM((rows_all, D), F32),
+        pltpu.VMEM((rows_all, D), F32),
+        pltpu.VMEM((rows_all, D), BF16),
+        pltpu.VMEM((half, D), BF16),
+        pltpu.VMEM((half, D), BF16),
+        pltpu.VMEM((half, D), F32),
+        pltpu.VMEM((rows_all, D), BF16),
+        pltpu.VMEM((rows_all, width), BF16),
+        pltpu.VMEM((half, D), BF16),
+        pltpu.VMEM((half, D), BF16),
+        pltpu.VMEM((2, experts) + grid + (shard, hidden), BF16),
+        pltpu.VMEM((experts, 2, 4, 2, shard, hidden), BF16),
+        pltpu.VMEM((experts, 2, 4, shard, hidden), BF16),
+        pltpu.VMEM((experts, 3, 2, shard, hidden), BF16),
+        pltpu.VMEM((4,) + grid + (shard, width), BF16),
+        pltpu.VMEM((4,) + grid + (shard, width), BF16),
+        pltpu.VMEM((2, 2, 4, 2, shard, width), BF16),
+        pltpu.VMEM((2, 2, 4, shard, width), BF16),
+        pltpu.VMEM((3, 4, shard, width), BF16),
+        pltpu.VMEM((4, 24, D), F32),
+        pltpu.VMEM((7, 24, D), F32),
+        pltpu.VMEM((4, 8, 128), F32),
+        pltpu.VMEM((7, 8, 128), F32),
+        dma((experts, 7)),
+        dma((experts, 7)),
+        dma((experts, 7)),
+        dma((experts, 7)),
+        dma((7,)),
+        dma((7,)),
+        dma((7,)),
+        dma((7,)),
+        dma((4,)),
+        dma((4,)),
+        dma((blocks,)),
+        dma((blocks,)),
+        dma((blocks,)),
+        dma((blocks,)),
+        dma((6,)),
+        dma((6,)),
+        dma((6,)),
+        dma((6,)),
+        dma((2,)),
+    ]
+    return pl.pallas_call(
+        step_kernel,
+        out_shape=outs,
+        in_specs=[vmem, vmem, pl.BlockSpec(memory_space=pltpu.SMEM)] + [vmem] * 7,
+        out_specs=[vmem] * 6 + [pl.BlockSpec(memory_space=pl.ANY)],
+        scratch_shapes=scratch,
+        compiler_params=pltpu.CompilerParams(
+            collective_id=0, has_side_effects=True, vmem_limit_bytes=64 << 20
+        ),
+        name="step",
+    )(x_rows, cotangent, task_ids, routes, norms, qkv, wo, router, win, wout)
+
+
 def shards(
     x_rows,
     cotangent,
@@ -402,9 +1207,120 @@
     )
 
 
+def shards_fused(
+    x_rows,
+    cotangent,
+    task_ids,
+    routes,
+    norm_params,
+    norm_first,
+    norm_second,
+    norm_ema,
+    qkv_weight,
+    qkv_first,
+    qkv_second,
+    qkv_ema,
+    out_weight,
+    out_first,
+    out_second,
+    out_ema,
+    router,
+    router_first,
+    router_second,
+    router_ema,
+    expert_in,
+    expert_in_first,
+    expert_in_second,
+    expert_in_ema,
+    expert_out,
+    expert_out_first,
+    expert_out_second,
+    expert_out_ema,
+):
+    output, input_grad, expert_red, qkvo_red, small, squares, unused = step_call(
+        x_rows,
+        cotangent,
+        task_ids,
+        routes,
+        norm_params,
+        qkv_weight,
+        out_weight,
+        router,
+        expert_in,
+        expert_out,
+    )
+    in_reduced, eout_reduced = expert_red[0], expert_red[1]
+    qkv_reduced, out_reduced = qkvo_red[0:3], qkvo_red[3]
+    norm_grad = small[0:4]
+    router_grad = jnp.concatenate([small[8:16].T, small[16:24, 0:TASKS].T], axis=0)
+    total_squares = squares[0, 0]
+    grad_norm = jnp.sqrt(total_squares)
+    clip_scale = jnp.minimum(1.0, CLIP_LIMIT / (grad_norm + 1e-06))
+    norm_new, norm_first_new, norm_second_new, norm_ema_new = adam_update(
+        norm_params, norm_first, norm_second, norm_ema, norm_grad, clip_scale, NORM_RATE
+    )
+    qkv_new, qkv_first_new, qkv_second_new, qkv_ema_new = adam_update(
+        qkv_weight, qkv_first, qkv_second, qkv_ema, qkv_reduced, clip_scale, LEARN_RATE
+    )
+    out_new, out_first_new, out_second_new, out_ema_new = adam_update(
+        out_weight, out_first, out_second, out_ema, out_reduced, clip_scale, LEARN_RATE
+    )
+    router_new, router_first_new, router_second_new, router_ema_new = adam_update(
+        router, router_first, router_second, router_ema, router_grad, clip_scale, LEARN_RATE
+    )
+    in_new, in_first_new, in_second_new, in_ema_new = adam_update(
+        expert_in,
+        expert_in_first,
+        expert_in_second,
+        expert_in_ema,
+        in_reduced,
+        clip_scale,
+        LEARN_RATE,
+    )
+    eout_new, eout_first_new, eout_second_new, eout_ema_new = adam_update(
+        expert_out,
+        expert_out_first,
+        expert_out_second,
+        expert_out_ema,
+        eout_reduced,
+        clip_scale,
+        LEARN_RATE,
+    )
+    return (
+        output,
+        input_grad,
+        grad_norm.reshape(1),
+        norm_new,
+        norm_first_new,
+        norm_second_new,
+        norm_ema_new,
+        qkv_new,
+        qkv_first_new,
+        qkv_second_new,
+        qkv_ema_new,
+        out_new,
+        out_first_new,
+        out_second_new,
+        out_ema_new,
+        router_new,
+        router_first_new,
+        router_second_new,
+        router_ema_new,
+        in_new,
+        in_first_new,
+        in_second_new,
+        in_ema_new,
+        eout_new,
+        eout_first_new,
+        eout_second_new,
+        eout_ema_new,
+    )
+
+
 def solution(mesh):
+    fused = mesh.shape["dp"] == GRID_Z * GRID_Y * GRID_X and mesh.shape["mp"] == 2
     return jax.shard_map(
-        shards,
+        shards_fused if fused else shards,
         mesh=mesh,
         in_specs=(
             P(("dp", "mp"), None),

time: 1760 us -> 270 us (0.15)
  waiting for transfers between devices: 645 us -> 0 us
  local copies, waits for them, and re-layouts: 323 us -> 8.8 us
  other arithmetic: 312 us -> 11.1 us
  matrix products: 280 us -> 0 us
  Pallas kernels: 0 us -> 247 us
  blocking collectives: 163 us -> 0 us
  between operations: 23.1 us -> 3.21 us
    reduce_scatter x7 -> x0, waiting for transfers between devices: 431 us -> none  [the longest x1 174 us: shards(): lax.psum_scatter(grad_eout_stack, 'dp', scatter_dimension=1, tiled=True)]
    dot_general x84 -> x0, matrix products: 280 us -> none  [the longest x8 37.6 us: expert_backward(): jnp.dot(grad_produced, weight_out, preferred_element_type=jnp.float32)]
    gather x34 -> x0, local copies, waits for them, and re-layouts: 247 us -> none  [the longest x1 68.5 us: shards(): slot_gate = gate_padded[slot_pair].reshape(E, CAP)]
    pallas_call x0 -> x1, Pallas kernels: none -> 247 us  [step_call(): pl.pallas_call(step_kernel, out_shape=outs, in_specs=[vmem, vmem, pl.Bloc...]
    scatter-add x16 -> x0, other arithmetic: 221 us -> none  [the longest x8 113 us: expert_backward(): carry.at[owners].add(grad_dispatched)]
    unnamed x15 -> x0, waiting for transfers between devices: 122 us -> none
    all_gather x6 -> x0, waiting for transfers between devices: 92.7 us -> none  [the longest x1 82.2 us: shards(): lax.all_gather(expert_out.astype(jnp.bfloat16), 'dp', axis=1, tiled=True)]
    all_gather x2 -> x0, blocking collectives: 82.1 us -> none  [the longest x1 43.5 us: shards(): lax.all_gather(out_weight.astype(jnp.bfloat16), 'dp', axis=0, tiled=True)]
  transfers between devices with their start and end apart: 14 -> 0, of which waited for: 9 -> 0; matrix products, arithmetic and copies ran while one was open for 19% -> 0% of each run, Pallas kernels for 0% -> 0%
where the time goes in v1:
time: 270 us
  Pallas kernels  247 us (91%)
  other arithmetic  11.1 us (4%)
  local copies, waits for them, and re-layouts  8.8 us (3%)
  between operations  3.21 us (1%)
    pallas_call x1, Pallas kernels, step_call(): pl.pallas_call(step_kernel, out_shape=outs, in_specs=[vmem, vmem, pl.Bloc...  247 us
    add x5, other arithmetic, adam_update(): average_new = EMA_KEEP * average + (1.0 - EMA_KEEP) * weight_new  11.1 us
    unnamed x10, local copies, waits for them, and re-layouts  6.16 us

profile of v1, /device:TPU:0, one launch (start us, length us, event | category | flops | bytes accessed | tf_op | source)
XLA Modules:
  0.0 269.7 jit_solution(11378465983998406694)
XLA Ops:
  1.3 1.5 copy.56.router_ref
  2.8 1.9 copy.55.routes_ref
  4.8 246.6 %step.1 = (f32[768,384]{1,0:T(8,128)}, f32[768,384]{1,0:T(8,128)}, f32[2,8,24,768]{3,2,1,0:T(8,128)}, f32[4,24,192]{2,1,0:T(8,128)}, f32[24,384]{1,0:T(8,128)}, ...) custom-call(bf16[768,384]{1,0:T(8,128)(2,1)} %x_ref.1, f32[768,384]{1,0:T(8,128)} %cot_ref.1, s32[1]{0:T(128)S(6)} %copy.59.task_ref, ...), custom_call_target="tpu_custom_call" | custom-call | tf_op jit(solution)/shard_map/step/pallas_call | solution.py:938
  251.3 0.0 copy-start
  251.3 1.3 slice.24
  253.3 0.7 slice_bitcast_fusion.1
  254.0 0.7 slice_bitcast_fusion
  254.7 1.4 multiply_add_fusion.7
  256.1 1.4 multiply_add_fusion.5
  257.5 1.5 multiply_add_fusion.4
  259.0 1.8 multiply_add_fusion.2
  260.7 0.0 copy-done
  260.7 0.0 copy-start.2
  260.7 5.1 %multiply_add_fusion = (f32[8,24,768]{2,1,0:T(8,128)}, f32[8,24,768]{2,1,0:T(8,128)}, f32[8,24,768]{2,1,0:T(8,128)}, f32[8,24,768]{2,1,0:T(8,128)}, f32[8,24,768...) fusion(f32[8,24,768]{2,1,0:T(8,128)} %param.55, f32[8,24,768]{2,1,0:T(8,128)} %wout_ref.1, ...), kind=kLoop, calls=%fused_computation.8 | loop fusion | flops 5603328 | bytes 10616836 | tf_op jit(solution)/shard_map/add | solution.py:144
  265.9 0.0 copy-done.2
  265.9 0.0 copy-start.1
  265.9 1.0 copy.60
  266.9 0.7 copy-done.1
  267.6 1.0 copy.61
Async XLA Ops:
  251.3 9.4 %copy-start = (f32[8,24,768]{2,1,0:T(8,128)S(1)}, f32[8,24,768]{2,1,0:T(8,128)}, u32[]{:S(2)}) copy-start(f32[8,24,768]{2,1,0:T(8,128)} %win_ref.1) | copy-start | bytes 1769476
  260.7 5.1 %copy-start.2 = (f32[768,384]{1,0:T(8,128)S(1)}, f32[768,384]{1,0:T(8,128)}, u32[]{:S(2)}) copy-start(f32[768,384]{1,0:T(8,128)} %get-tuple-element.94) | copy-start | bytes 3538948
  265.9 1.7 copy-start.1

commit v2 on v1

--- a/solution.py
+++ b/solution.py
@@ -152,6 +152,7 @@
 NN = ((1,), (0,))
 NT = ((1,), (1,))
 TN = ((0,), (0,))
+TT = ((0,), (1,))
 GRID_Z, GRID_Y, GRID_X = 4, 2, 2
 ROW_BLOCK = 256
 
@@ -188,7 +189,7 @@
     red_ref,
     redq_ref,
     small_ref,
-    sumsq_ref,
+    late_ref,
     p_hbm,
     x_sib,
     g_all,
@@ -202,30 +203,35 @@
     mid,
     x2,
     gates,
-    wgt,
+    wgt_t,
     mix,
     gsec,
     gs_r,
     mix_s,
     mix_r,
-    gm_own,
-    gml,
     gctx,
-    gfirst_s,
     gfirst_r,
+    pair_s,
+    pair_r,
+    back_r,
     gw,
+    gd,
+    wsend,
     r1,
     r2,
     r3,
+    r4,
     gq,
     gg,
     q1,
     q2,
     q3,
     ar_s,
-    ar_r,
-    sc_s,
-    sc_r,
+    ar_g,
+    ar_z,
+    la_s,
+    la_g,
+    la_z,
     ag_ss,
     ag_rs,
     rs_ss,
@@ -236,75 +242,81 @@
     gr_rs,
     sib_ss,
     sib_rs,
+    near_ss,
+    near_rs,
+    x2_ss,
+    x2_rs,
+    x2f_ss,
+    x2f_rs,
     att_ss,
     att_rs,
     gs_ss,
     gs_rs,
     ar_ss,
     ar_rs,
-    sc_ss,
-    sc_rs,
+    la_ss,
+    la_rs,
     p_sem,
+    in_sem,
 ):
     experts = win_ref.shape[0]
+    local = experts // 2
     half = x_ref.shape[0]
     rows_all = 2 * half
     width = qs.shape[1]
+    hidden_width = gw.shape[-1]
     heads = width // HD
     tb = ROW_BLOCK
     blocks = rows_all // tb
     own_blocks = half // tb
+    pshape = (2, heads, tb, rows_all)
+    wshape = gw.shape[2:]
+    qshape = gg.shape[1:]
 
     d = lax.axis_index("dp")
     m = lax.axis_index("mp")
     z = d // 4
     y = (d // 2) % 2
     x = d % 2
+    zg = z // 2
+    zl = z % 2
+    zp = z + 1 - 2 * zl
     sib = (d, 1 - m)
     xn = (d + 1 - 2 * x, m)
     yn = (d + 2 - 4 * y, m)
+    near = (zp * 4 + y * 2 + x, m)
+    far = ((z + 2 - 4 * zg) * 4 + y * 2 + x, m)
     zs = [((z + k) % 4) for k in (1, 2, 3)]
     zn = [(zs[k] * 4 + y * 2 + x, m) for k in range(3)]
+    base = zl * local
+    other = (1 - zl) * local
+
+    load_in = pltpu.make_async_copy(win_ref, red_ref.at[0], in_sem.at[0])
+    load_out = pltpu.make_async_copy(wout_ref, red_ref.at[1], in_sem.at[1])
+    load_cot = pltpu.make_async_copy(cot_ref, igrad_ref, in_sem.at[2])
+    for c in [load_in, load_out, load_cot]:
+        c.start()
 
     barrier = pltpu.get_barrier_semaphore()
-    for peer in [sib, xn, yn] + zn:
+    plane = [
+        (
+            z * 4 + (y + a * (1 - 2 * y)) * 2 + (x + b * (1 - 2 * x)),
+            m + c * (1 - 2 * m),
+        )
+        for a in (0, 1)
+        for b in (0, 1)
+        for c in (0, 1)
+        if a + b + c > 0
+    ]
+    for peer in plane + zn:
         pl.semaphore_signal(barrier, inc=1, device_id=peer, device_id_type=MESH)
-    pl.semaphore_wait(barrier, 6)
+    pl.semaphore_wait(barrier, 10)
 
     def rcopy(src, dst, ss, rs, dev):
         return pltpu.make_async_remote_copy(
             src_ref=src, dst_ref=dst, send_sem=ss, recv_sem=rs, device_id=dev, device_id_type=MESH
         )
 
-    def own_rows(b):
-        return pl.ds(pl.multiple_of(m * half + b * tb, tb), tb)
-
-    def sib_rows(b):
-        return pl.ds(pl.multiple_of((1 - m) * half + b * tb, tb), tb)
-
-    def blk_rows(b):
-        return pl.ds(pl.multiple_of(b * tb, tb), tb)
-
-    own_half = pl.ds(pl.multiple_of(m * half, half), half)
-
-    def ag1(e):
-        return [
-            rcopy(gw.at[:, e, z, y, x], gw.at[:, e, z, y, x], ag_ss.at[e, k], ag_rs.at[e, k], zn[k])
-            for k in range(3)
-        ]
-
-    def ag2(e):
-        return [
-            rcopy(gw.at[0, e, :, y, x], gw.at[0, e, :, y, x], ag_ss.at[e, 3], ag_rs.at[e, 3], xn),
-            rcopy(gw.at[1, e, :, y, x], gw.at[1, e, :, y, x], ag_ss.at[e, 4], ag_rs.at[e, 4], yn),
-        ]
-
-    def ag3(e):
-        return [
-            rcopy(gw.at[0, e, :, y], gw.at[0, e, :, y], ag_ss.at[e, 5], ag_rs.at[e, 5], yn),
-            rcopy(gw.at[1, e, :, :, x], gw.at[1, e, :, :, x], ag_ss.at[e, 6], ag_rs.at[e, 6], xn),
-        ]
-
     def start(copies):
         for c in copies:
             c.start()
@@ -317,76 +329,96 @@
         for c in copies:
             c.wait_send()
 
+    def blk_rows(b):
+        return pl.ds(pl.multiple_of(b * tb, tb), tb)
+
+    def own_rows(b):
+        return pl.ds(pl.multiple_of(m * half + b * tb, tb), tb)
+
+    def sib_rows(b):
+        return pl.ds(pl.multiple_of((1 - m) * half + b * tb, tb), tb)
+
+    own_half = pl.ds(pl.multiple_of(m * half, half), half)
+
+    zpair = pl.ds(zg * 2, 2)
+    zaway = pl.ds((1 - zg) * 2, 2)
+
+    def ag0(i):
+        return [
+            rcopy(wsend.at[:, i], gw.at[:, i, z, y, x], ag_ss.at[i, 0], ag_rs.at[i, 0], near)
+        ]
+
+    def ag1(i):
+        part = gw.at[:, i, zpair, y, x]
+        return [rcopy(part, part, ag_ss.at[i, 1], ag_rs.at[i, 1], far)]
+
+    def ag2(i):
+        return [
+            rcopy(gw.at[0, i, :, y, x], gw.at[0, i, :, y, x], ag_ss.at[i, 2], ag_rs.at[i, 2], xn),
+            rcopy(gw.at[1, i, :, y, x], gw.at[1, i, :, y, x], ag_ss.at[i, 3], ag_rs.at[i, 3], yn),
+        ]
+
+    def ag3(i):
+        return [
+            rcopy(gw.at[0, i, :, y], gw.at[0, i, :, y], ag_ss.at[i, 4], ag_rs.at[i, 4], yn),
+            rcopy(gw.at[1, i, :, :, x], gw.at[1, i, :, :, x], ag_ss.at[i, 5], ag_rs.at[i, 5], xn),
+        ]
+
     def ag_tick(t):
-        @pl.when(jnp.logical_and(t >= 0, t < experts))
-        def _():
-            arrive(ag1(t))
-            start(ag2(t))
-
-        @pl.when(t + 2 < experts)
-        def _():
-            start(ag1(t + 2))
-
-        @pl.when(jnp.logical_and(t >= 1, t < experts + 1))
-        def _():
-            arrive(ag2(t - 1))
-            start(ag3(t - 1))
-
-        @pl.when(jnp.logical_and(t >= 2, t < experts + 2))
-        def _():
-            arrive(ag3(t - 2))
-
-    def rs1(e):
+        if 0 <= t < local:
+            arrive(ag0(t))
+            start(ag1(t))
+        if 0 <= t - 1 < local:
+            arrive(ag1(t - 1))
+            start(ag2(t - 1))
+        if 0 <= t - 2 < local:
+            arrive(ag2(t - 2))
+            start(ag3(t - 2))
+
+    def rs1(i):
         return [
-            rcopy(gw.at[0, e, :, 1 - y], r1.at[e, 0], rs_ss.at[e, 0], rs_rs.at[e, 0], yn),
-            rcopy(gw.at[1, e, :, :, 1 - x], r1.at[e, 1], rs_ss.at[e, 1], rs_rs.at[e, 1], xn),
+            rcopy(gd.at[0, i, :, 1 - y], r1.at[i, 0], rs_ss.at[i, 0], rs_rs.at[i, 0], yn),
+            rcopy(gd.at[1, i, :, :, 1 - x], r1.at[i, 1], rs_ss.at[i, 1], rs_rs.at[i, 1], xn),
         ]
 
-    def rs2(e):
+    def rs2(i):
         return [
-            rcopy(gw.at[0, e, :, y, 1 - x], r2.at[e, 0], rs_ss.at[e, 2], rs_rs.at[e, 2], xn),
-            rcopy(gw.at[1, e, :, 1 - y, x], r2.at[e, 1], rs_ss.at[e, 3], rs_rs.at[e, 3], yn),
+            rcopy(gd.at[0, i, :, y, 1 - x], r2.at[i, 0], rs_ss.at[i, 2], rs_rs.at[i, 2], xn),
+            rcopy(gd.at[1, i, :, 1 - y, x], r2.at[i, 1], rs_ss.at[i, 3], rs_rs.at[i, 3], yn),
         ]
 
-    def rs3(e):
+    def rs3(i):
         return [
-            rcopy(
-                gw.at[:, e, zs[k], y, x], r3.at[e, k], rs_ss.at[e, 4 + k], rs_rs.at[e, 4 + k], zn[k]
-            )
-            for k in range(3)
+            rcopy(gd.at[:, i, zaway, y, x], r3.at[i], rs_ss.at[i, 4], rs_rs.at[i, 4], far)
         ]
 
-    def rs_tick(t):
-        @pl.when(jnp.logical_and(t >= 0, t < experts))
-        def _():
-            start(rs1(t))
-
-        @pl.when(jnp.logical_and(t >= 1, t < experts + 1))
-        def _():
-            e = t - 1
-            arrive(rs1(e))
-            gw[0, e, :, y] = (gw[0, e, :, y].astype(F32) + r1[e, 0].astype(F32)).astype(BF16)
-            gw[1, e, :, :, x] = (gw[1, e, :, :, x].astype(F32) + r1[e, 1].astype(F32)).astype(BF16)
-            start(rs2(e))
-
-        @pl.when(jnp.logical_and(t >= 2, t < experts + 2))
-        def _():
-            e = t - 2
-            arrive(rs2(e))
-            for a in range(2):
-                gw[a, e, :, y, x] = (
-                    gw[a, e, :, y, x].astype(F32) + r2[e, a].astype(F32)
-                ).astype(BF16)
-            start(rs3(e))
-
-        @pl.when(jnp.logical_and(t >= 3, t < experts + 3))
-        def _():
-            e = t - 3
-            arrive(rs3(e))
-            total = gw[:, e, z, y, x].astype(F32)
-            for k in range(3):
-                total = total + r3[e, k].astype(F32)
-            red_ref[:, e] = total
+    def rs4(i):
+        return [rcopy(gd.at[:, i, zp, y, x], r4.at[i], rs_ss.at[i, 5], rs_rs.at[i, 5], near)]
+
+    def add_low(one, two):
+        return (one.astype(F32) + two.astype(F32)).astype(BF16)
+
+    def rs_b(i):
+        arrive(rs1(i))
+        gd[0, i, :, y] = add_low(gd[0, i, :, y], r1[i, 0])
+        gd[1, i, :, :, x] = add_low(gd[1, i, :, :, x], r1[i, 1])
+        start(rs2(i))
+
+    def rs_c(i):
+        arrive(rs2(i))
+        for a in range(2):
+            gd[a, i, :, y, x] = add_low(gd[a, i, :, y, x], r2[i, a])
+        start(rs3(i))
+
+    def rs_d(i):
+        arrive(rs3(i))
+        red_ref[:, base + i] = gd[:, i, z, y, x].astype(F32) + r3[i, :, zl].astype(F32)
+        gd[:, i, zp, y, x] = add_low(gd[:, i, zp, y, x], r3[i, :, 1 - zl])
+        start(rs4(i))
+
+    def rs_e(i):
+        arrive(rs4(i))
+        red_ref[:, other + i] = r4[i].astype(F32)
 
     gq1 = [
         rcopy(gq.at[:, z, y, x], gq.at[:, z, y, x], gq_ss.at[k], gq_rs.at[k], zn[k])
@@ -414,29 +446,85 @@
     ]
 
     send_x = rcopy(x_ref, x_sib, sib_ss.at[0], sib_rs.at[0], sib)
+    own_g = g_all.at[0, own_half]
+    pair_g = g_all.at[1, own_half]
+    send_g = rcopy(own_g, own_g, sib_ss.at[1], sib_rs.at[1], sib)
+    near_g = rcopy(own_g, pair_g, near_ss.at[0], near_rs.at[0], near)
+    pass_g = rcopy(pair_g, pair_g, sib_ss.at[2], sib_rs.at[2], sib)
+    near_gates = rcopy(gates.at[0], gates.at[1], near_ss.at[1], near_rs.at[1], near)
+
+    def near_x2(b):
+        r = own_rows(b)
+        return rcopy(x2.at[0, r], x2.at[1, r], x2_ss.at[b], x2_rs.at[b], near)
+
+    def pass_x2(b):
+        r = own_rows(b)
+        return rcopy(x2.at[1, r], x2.at[1, r], x2f_ss.at[b], x2f_rs.at[b], sib)
+
+    pair_copies = [
+        rcopy(pair_s.at[k], pair_r.at[k], sib_ss.at[3 + k], sib_rs.at[3 + k], sib)
+        for k in range(2)
+    ]
+    back_copies = [
+        rcopy(x_sib, back_r.at[0], near_ss.at[2], near_rs.at[2], near),
+        rcopy(mix_s, back_r.at[1], near_ss.at[3], near_rs.at[3], near),
+    ]
+    send_mix = rcopy(pair_s.at[1], mix_r, sib_ss.at[5], sib_rs.at[5], sib)
+    send_first = rcopy(pair_s.at[0], gfirst_r, sib_ss.at[6], sib_rs.at[6], sib)
+
+    place = (y * 2 + x) * 2 + m
+
+    class SumAll:
+        def __init__(self, src, group, line, ss, rs):
+            self.src, self.group, self.line = src, group, line
+            self.near = [
+                rcopy(src.at[0], group.at[place], ss.at[k], rs.at[k], plane[k]) for k in range(7)
+            ]
+            self.along = [
+                rcopy(src.at[1], line.at[z], ss.at[7 + k], rs.at[7 + k], zn[k]) for k in range(3)
+            ]
+
+        def one(self):
+            start(self.near)
+            self.group[place] = self.src[0]
+
+        def two(self):
+            arrive(self.near)
+            total = self.group[0]
+            for k in range(1, 8):
+                total = total + self.group[k]
+            self.src[1] = total
+            start(self.along)
+            self.line[z] = total
+
+        def three(self):
+            arrive(self.along)
+            return (self.line[0] + self.line[1]) + (self.line[2] + self.line[3])
+
+        def done(self):
+            sent(self.near + self.along)
+
+    early = SumAll(ar_s, ar_g, ar_z, ar_ss, ar_rs)
+    late = SumAll(la_s, la_g, la_z, la_ss, la_rs)
+
     send_x.start()
     for c in range(3):
         gq[c, z, y, x] = qkv_ref[c].astype(BF16)
     gq[3, z, y, x] = wo_ref[...].astype(BF16)
     start(gq1)
 
-    def cast_weights(e, carry):
-        gw[0, e, z, y, x] = win_ref[e].astype(BF16)
-        gw[1, e, z, y, x] = wout_ref[e].astype(BF16)
+    load_in.wait()
+    load_out.wait()
+
+    def cast_weights(i, carry):
+        for a in range(2):
+            wsend[a, i] = red_ref[a, other + i].astype(BF16)
+        start(ag0(i))
+        for a in range(2):
+            gw[a, i, z, y, x] = red_ref[a, base + i].astype(BF16)
         return carry
 
-    lax.fori_loop(0, 2, cast_weights, 0)
-    start(ag1(0))
-    start(ag1(1))
-    lax.fori_loop(2, experts, cast_weights, 0)
-
-    def cast_cot(b, carry):
-        g_all[own_rows(b), :] = cot_ref[blk_rows(b), :].astype(BF16)
-        return carry
-
-    lax.fori_loop(0, own_blocks, cast_cot, 0)
-    send_g = rcopy(g_all.at[own_half], g_all.at[own_half], sib_ss.at[1], sib_rs.at[1], sib)
-    send_g.start()
+    lax.fori_loop(0, local, cast_weights, 0)
 
     gain1 = norm_ref[0:1, :]
     bias1 = norm_ref[1:2, :]
@@ -458,11 +546,20 @@
     lax.fori_loop(0, own_blocks, first_own, 0)
     arrive(gq1)
     start(gq2)
+    ag_tick(0)
     send_x.wait_recv()
     lax.fori_loop(0, own_blocks, first_sib, 0)
     arrive(gq2)
     start(gq3)
-    ag_tick(jnp.int32(0))
+
+    def cast_cot(b, carry):
+        g_all[0, own_rows(b), :] = igrad_ref[blk_rows(b), :].astype(BF16)
+        return carry
+
+    load_cot.wait()
+    lax.fori_loop(0, own_blocks, cast_cot, 0)
+    send_g.start()
+    ag_tick(1)
     arrive(gq3)
 
     def flat(c):
@@ -507,14 +604,15 @@
             ctx[r, :] = context
             att_s[r, :] = mm(context, flat(3), NT).astype(BF16)
             att_copy(b).start()
-
-            @pl.when(b == 1)
+            @pl.when(b == 3)
             def _():
-                ag_tick(jnp.int32(1))
-
-            @pl.when(b == 4)
-            def _():
-                ag_tick(jnp.int32(2))
+                near_g.start()
+
+            for t, when in ((2, 0), (3, 2), (4, 4)):
+
+                @pl.when(b == when)
+                def _(t=t):
+                    ag_tick(t)
 
             return carry
 
@@ -522,18 +620,20 @@
         p_out(blocks - 2).wait()
         p_out(blocks - 1).wait()
 
-
-    pshape = (2, heads, tb, rows_all)
     pl.run_scoped(attention, pltpu.VMEM(pshape, BF16))
-
-    router_main = router_ref[0:D, :]
-    router_hi = router_main.astype(BF16)
-    router_lo = (router_main - router_hi.astype(F32)).astype(BF16)
+    ag_tick(5)
+
+    router_t = router_ref[:, 0:D]
+    router_hi = router_t.astype(BF16)
+    router_lo = (router_t - router_hi.astype(F32)).astype(BF16)
     task = task_ref[0]
-    n_tasks = router_ref.shape[0] - D
-    task_pick = lax.broadcasted_iota(jnp.int32, (n_tasks, experts), 0) == task
-    task_bias = jnp.sum(jnp.where(task_pick, router_ref[D:, :], 0.0), axis=0, keepdims=True)
-    lane = lax.broadcasted_iota(jnp.int32, (tb, experts), 1)
+    n_tasks = router_ref.shape[1] - D
+    task_lanes = lax.broadcasted_iota(jnp.int32, (experts, n_tasks), 1)
+    task_bias = jnp.sum(
+        jnp.where(task_lanes == task, router_ref[:, D:], 0.0), axis=1, keepdims=True
+    )
+    row_id = lax.broadcasted_iota(jnp.int32, (experts, tb), 0)
+    gates[0, experts : 2 * experts, :] = jnp.full((experts, rows_all), task.astype(F32), F32)
 
     def second_norm(rows, source, b, gb):
         att_copy(gb).wait_recv()
@@ -545,18 +645,19 @@
         mid[rows, :] = rows_mid
         unit, _ = row_stats(rows_mid)
         normed = (unit * gain2 + bias2).astype(BF16)
-        x2[rows, :] = normed
-        logits = mm(normed, router_hi) + mm(normed, router_lo) + task_bias
-        picks = routes_ref[rows, :]
-        chosen = lane == picks[:, 0:1]
+        x2[0, rows, :] = normed
+        logits = mm(router_hi, normed, NT) + mm(router_lo, normed, NT) + task_bias
+        chosen = row_id == routes_ref[0:1, rows]
         for k in range(1, TOP):
-            chosen = jnp.logical_or(chosen, lane == picks[:, k : k + 1])
-        peak = jnp.max(jnp.where(chosen, logits, -jnp.inf), axis=1, keepdims=True)
+            chosen = jnp.logical_or(chosen, row_id == routes_ref[k : k + 1, rows])
+        peak = jnp.max(jnp.where(chosen, logits, -jnp.inf), axis=0, keepdims=True)
         powers = jnp.where(chosen, jnp.exp(logits - peak), 0.0)
-        gates[rows, :] = powers / jnp.sum(powers, axis=1, keepdims=True)
+        share = powers / jnp.sum(powers, axis=0, keepdims=True)
+        gates[0, 0:experts, rows] = share
 
     def second_own(b, carry):
         second_norm(own_rows(b), x_ref, b, m * own_blocks + b)
+        near_x2(b).start()
         return carry
 
     def second_sib(b, carry):
@@ -565,30 +666,144 @@
 
     lax.fori_loop(0, own_blocks, second_own, 0)
     lax.fori_loop(0, own_blocks, second_sib, 0)
+    near_gates.start()
     send_g.wait_recv()
-    ag_tick(jnp.int32(3))
 
     def clear(b, carry):
         r = blk_rows(b)
-        mix[r, :] = jnp.zeros((tb, D), F32)
-        gsec[r, :] = jnp.zeros((tb, D), F32)
-        wgt[r, :] = jnp.zeros((tb, experts), F32)
+        for st in range(2):
+            mix[st, r, :] = jnp.zeros((tb, D), F32)
+            gsec[st, r, :] = jnp.zeros((tb, D), F32)
         return carry
 
     lax.fori_loop(0, blocks, clear, 0)
+    wgt_t[...] = jnp.zeros(wgt_t.shape, F32)
+
+    def gate_grad(st, share_all, rows):
+        share = wgt_t[st, :, rows]
+        grad_logits = share - share_all * jnp.sum(share, axis=0, keepdims=True)
+        high = grad_logits.astype(BF16)
+        low = (grad_logits - high.astype(F32)).astype(BF16)
+        normed = x2[st, rows, :]
+        rg = mm(high, normed) + mm(low, normed)
+        tg = jnp.sum(grad_logits, axis=1, keepdims=True)
+        return gsec[st, rows, :] + mm(high, router_hi, TN), rg, tg
+
+    def pair_rows_in():
+        near_gates.wait_recv()
+        pass_g.wait_recv()
+
+        def land(b, carry):
+            pass_x2(b).wait_recv()
+            return carry
+
+        lax.fori_loop(0, own_blocks, land, 0)
+
+    def pass_rows(b, carry):
+        near_x2(b).wait_recv()
+        pass_x2(b).start()
+        return carry
+
+    task_row = lax.broadcasted_iota(jnp.int32, (experts, 128), 1).astype(F32)
+
+    def pair_rows_out():
+        def keep(b, carry):
+            rg, tg = carry
+            rows = own_rows(b)
+            upstream, more_rg, more_tg = gate_grad(1, gates[1, 0:experts, rows], rows)
+            gsec[1, rows, :] = upstream
+            return rg + more_rg, tg + more_tg
+
+        def give(b, carry):
+            rg, tg = carry
+            rows = sib_rows(b)
+            upstream, more_rg, more_tg = gate_grad(1, gates[1, 0:experts, rows], rows)
+            pair_s[0, blk_rows(b), :] = upstream.astype(BF16)
+            pair_s[1, blk_rows(b), :] = mix[1, rows, :].astype(BF16)
+            return rg + more_rg, tg + more_tg
+
+        zero = (jnp.zeros((experts, D), F32), jnp.zeros((experts, 1), F32))
+        sums = lax.fori_loop(0, own_blocks, give, zero)
+        start(pair_copies)
+        rg, tg = lax.fori_loop(0, own_blocks, keep, sums)
+        ar_s[0] = jnp.zeros(ar_s.shape[1:], F32)
+        ar_s[0, 8:16, :] = rg
+        pair_task = gates[1, experts : experts + 1, 0:128]
+        ar_s[0, 16:24, 0:128] = jnp.where(task_row == pair_task, tg, 0.0)
+
+    def pair_rows_back():
+        arrive(pair_copies)
+
+        def grads(b, carry):
+            r = blk_rows(b)
+            x_sib[r, :] = (gsec[1, own_rows(b), :] + pair_r[0, r, :].astype(F32)).astype(BF16)
+            return carry
+
+        def rows(b, carry):
+            r = blk_rows(b)
+            mix_s[r, :] = (mix[1, own_rows(b), :] + pair_r[1, r, :].astype(F32)).astype(BF16)
+            return carry
+
+        lax.fori_loop(0, own_blocks, grads, 0)
+        back_copies[0].start()
+        lax.fori_loop(0, own_blocks, rows, 0)
+        back_copies[1].start()
 
     def all_experts(g_gate, hid, gpre):
-        def expert(e, carry):
-            ag_tick(e + 4)
-            rs_tick(e - 1)
+        def segment(s, carry):
+            pair = jnp.logical_and(s >= 2, s < 6)
+            st = jnp.where(pair, 1, 0)
+            i = s - jnp.where(s >= 6, 4, jnp.where(s >= 2, 2, 0))
+            e = base + i
+            first = jnp.logical_or(s < 2, jnp.logical_and(s >= 4, s < 6))
+
+            @pl.when(first)
+            def _():
+                arrive(ag3(i))
+
+            @pl.when(s == 1)
+            def _():
+                near_g.wait_recv()
+                pass_g.start()
+                lax.fori_loop(0, own_blocks, pass_rows, 0)
+
+            @pl.when(s == 2)
+            def _():
+                pair_rows_in()
+
+            @pl.when(s == 3)
+            def _():
+                start(rs1(0))
+
+            @pl.when(s == 4)
+            def _():
+                start(rs1(1))
+                rs_b(0)
+
+            @pl.when(s == 5)
+            def _():
+                rs_b(1)
+                rs_c(0)
+
+            @pl.when(s == 6)
+            def _():
+                pair_rows_out()
+                rs_c(1)
+                rs_d(0)
+
+            @pl.when(s == 7)
+            def _():
+                pair_rows_back()
+                start(rs1(2))
+                rs_d(1)
 
             def block(b, carry2):
                 r = blk_rows(b)
-                w_in = gw[0, e].reshape(D, gw.shape[-1])
-                w_out = gw[1, e].reshape(D, gw.shape[-1])
-                gate = jnp.sum(jnp.where(lane == e, gates[r, :], 0.0), axis=1, keepdims=True)
-                pre = mm(x2[r, :], w_in)
-                incoming = (gate * g_all[r, :].astype(F32)).astype(BF16)
+                w_in = gw[0, i].reshape(D, hidden_width)
+                w_out = gw[1, i].reshape(D, hidden_width)
+                gate = gates[st, pl.ds(e, 1), r].T
+                pre = mm(x2[st, r, :], w_in)
+                incoming = (gate * g_all[st, r, :].astype(F32)).astype(BF16)
                 g_gate[r, :] = incoming
                 grad_hidden = mm(incoming, w_out)
                 phi = 0.5 + 0.5 * lax.erf(pre * SQRT_HALF)
@@ -598,28 +813,37 @@
                 grad_pre = (grad_hidden * (phi + pre * density)).astype(BF16)
                 gpre[r, :] = grad_pre
                 produced = mm(hidden, w_out, NT)
-                mix[r, :] += gate * produced
+                mix[st, r, :] += gate * produced
                 weight = jnp.sum(incoming.astype(F32) * produced, axis=1, keepdims=True)
-                wgt[r, :] = jnp.where(lane == e, weight, wgt[r, :])
-                gsec[r, :] += mm(grad_pre, w_in, NT)
+                wgt_t[st, pl.ds(e, 1), r] = weight.T
+                gsec[st, r, :] += mm(grad_pre, w_in, NT)
                 return carry2
 
             lax.fori_loop(0, blocks, block, 0)
-            sent(ag1(e) + ag2(e) + ag3(e))
-            shape = gw.shape[2:]
-            gw[0, e] = mm(x2[...], gpre[...], TN).reshape(shape).astype(BF16)
-            gw[1, e] = mm(g_gate[...], hid[...], TN).reshape(shape).astype(BF16)
+
+            def keep_sum(a, value):
+                @pl.when(first)
+                def _():
+                    gd[a, i] = value.astype(BF16)
+
+                @pl.when(jnp.logical_not(first))
+                def _():
+                    gd[a, i] = (gd[a, i].astype(F32) + value).astype(BF16)
+
+            keep_sum(0, mm(x2[st], gpre[...], TN).reshape(wshape))
+            keep_sum(1, mm(g_gate[...], hid[...], TN).reshape(wshape))
             return carry
 
-        lax.fori_loop(0, experts, expert, 0)
+        lax.fori_loop(0, 2 * local, segment, 0)
 
     pl.run_scoped(
         all_experts,
         pltpu.VMEM((rows_all, D), BF16),
-        pltpu.VMEM((rows_all, gw.shape[-1]), BF16),
-        pltpu.VMEM((rows_all, gw.shape[-1]), BF16),
-    )
-    rs_tick(jnp.int32(experts - 1))
+        pltpu.VMEM((rows_all, hidden_width), BF16),
+        pltpu.VMEM((rows_all, hidden_width), BF16),
+    )
+    start(rs1(3))
+    rs_b(2)
 
     def gs_copy(b):
         r = blk_rows(b)
@@ -628,40 +852,40 @@
     for b in range(blocks):
         att_copy(b).wait_send()
 
-    ones = jnp.ones((tb, 128), BF16)
-
-    def gate_grad(b, carry):
+    def gate_sib(b, carry):
         rg, tg = carry
-        r = blk_rows(b)
-        share = wgt[r, :]
-        grad_logits = share - gates[r, :] * jnp.sum(share, axis=1, keepdims=True)
-        high = grad_logits.astype(BF16)
-        low = (grad_logits - high.astype(F32)).astype(BF16)
-        att_s[r, :] = (gsec[r, :] + mm(high, router_hi, NT)).astype(BF16)
-        gs_copy(b).start()
-        normed = x2[r, :]
-        rg = rg + mm(high, normed, TN) + mm(low, normed, TN)
-        tg = tg + mm(high, ones, TN) + mm(low, ones, TN)
-        return rg, tg
-
-    rg, tg = lax.fori_loop(
-        0,
-        blocks,
-        gate_grad,
-        (jnp.zeros((experts, D), F32), jnp.zeros((experts, 128), F32)),
-    )
-    task_lane = lax.broadcasted_iota(jnp.int32, (experts, 128), 1) == task
-    ar_s[0] = jnp.zeros(ar_s.shape[1:], F32)
-    ar_s[0, 8:16, :] = rg
-    ar_s[0, 16:24, 0:128] = jnp.where(task_lane, tg, 0.0)
+        rows = sib_rows(b)
+        upstream, more_rg, more_tg = gate_grad(0, gates[0, 0:experts, rows], rows)
+        att_s[rows, :] = upstream.astype(BF16)
+        gs_copy((1 - m) * own_blocks + b).start()
+        return rg + more_rg, tg + more_tg
+
+    def gate_own(b, carry):
+        rg, tg = carry
+        rows = own_rows(b)
+        upstream, more_rg, more_tg = gate_grad(0, gates[0, 0:experts, rows], rows)
+        att_s[rows, :] = (upstream + back_r[0, blk_rows(b), :].astype(F32)).astype(BF16)
+        gs_copy(m * own_blocks + b).start()
+        return rg + more_rg, tg + more_tg
+
+    sums = (jnp.zeros((experts, D), F32), jnp.zeros((experts, 1), F32))
+    sums = lax.fori_loop(0, own_blocks, gate_sib, sums)
+    back_copies[0].wait_recv()
+    rg, tg = lax.fori_loop(0, own_blocks, gate_own, sums)
+    ar_s[0, 8:16, :] += rg
+    ar_s[0, 16:24, 0:128] += jnp.where(task_row == task.astype(F32), tg, 0.0)
+
+    sent(pair_copies)
 
     def mix_out(b, carry):
-        mix_s[blk_rows(b), :] = mix[sib_rows(b), :].astype(BF16)
+        pair_s[1, blk_rows(b), :] = mix[0, sib_rows(b), :].astype(BF16)
         return carry
 
     lax.fori_loop(0, own_blocks, mix_out, 0)
-    send_mix = rcopy(mix_s, mix_r, sib_ss.at[2], sib_rs.at[2], sib)
     send_mix.start()
+
+    gml = att_r
+    w_o = flat(3)
 
     def back_second(rows, gb):
         gs_copy(gb).wait_recv()
@@ -670,14 +894,12 @@
         back = row_back(grad_second, unit, inv_std, gain2)
         return grad_second, unit, back
 
-    w_o = flat(3)
-
     def back_own(b, carry):
         gain_sum, bias_sum = carry
         rows = own_rows(b)
         grad_second, unit, back = back_second(rows, m * own_blocks + b)
-        grad_mid = cot_ref[blk_rows(b), :] + back
-        gm_own[blk_rows(b), :] = grad_mid
+        grad_mid = igrad_ref[blk_rows(b), :] + back
+        igrad_ref[blk_rows(b), :] = grad_mid
         grad_low = grad_mid.astype(BF16)
         gml[rows, :] = grad_low
         gctx[rows, :] = mm(grad_low, w_o).astype(BF16)
@@ -688,7 +910,7 @@
     def back_sib(b, carry):
         rows = sib_rows(b)
         grad_second, unit, back = back_second(rows, (1 - m) * own_blocks + b)
-        grad_low = (g_all[rows, :].astype(F32) + back).astype(BF16)
+        grad_low = (g_all[0, rows, :].astype(F32) + back).astype(BF16)
         gml[rows, :] = grad_low
         gctx[rows, :] = mm(grad_low, w_o).astype(BF16)
         return carry
@@ -697,11 +919,14 @@
     gain2_grad, bias2_grad = lax.fori_loop(0, own_blocks, back_own, (zero_row, zero_row))
     ar_s[0, 2:3, :] = gain2_grad
     ar_s[0, 3:4, :] = bias2_grad
+    early.one()
     lax.fori_loop(0, own_blocks, back_sib, 0)
-    qshape = gg.shape[1:]
     gg[3] = mm(gml[...], ctx[...], TN).reshape(qshape).astype(BF16)
 
-    def last_part(pbuf, keys_acc, values_acc, dq):
+    pass_g.wait_send()
+
+    def last_part(pbuf, keys_acc, values_acc):
+
         def p_in(b):
             return pltpu.make_async_copy(p_hbm.at[b], pbuf.at[b % 2], p_sem.at[b % 2])
 
@@ -730,99 +955,105 @@
                 outs.append(mm(grad_scores, ks[:, cs]) * SCORE_SCALE)
                 keys_acc[cs, :] += mm(qs[r, cs], grad_scores, TN)
                 values_acc[cs, :] += mm(grad_block, prob, TN)
-            dq[r, :] = jnp.concatenate(outs, axis=1).astype(BF16)
-            rs_tick(b + experts)
+            g_all[1, r, 0:width] = jnp.concatenate(outs, axis=1).astype(BF16)
+
+            @pl.when(b == 0)
+            def _():
+                rs_b(3)
+                rs_c(2)
+
+            @pl.when(b == 2)
+            def _():
+                rs_c(3)
+                rs_d(2)
+                early.two()
+
+            @pl.when(b == 4)
+            def _():
+                rs_d(3)
+                rs_e(0)
+                rs_e(1)
+                small_ref[...] = early.three()
+
             return carry
 
         lax.fori_loop(0, blocks, attend_back, 0)
 
-        send_mix.wait_recv()
-
-        def write_out(b, carry):
-            r = blk_rows(b)
-            rows = own_rows(b)
-            out_ref[r, :] = mid[rows, :] + mix[rows, :] + mix_r[r, :].astype(F32)
-            return carry
-
-        lax.fori_loop(0, own_blocks, write_out, 0)
-
         normed = x1[...]
-        gg[0] = mm(normed, dq[...], TN).reshape(qshape).astype(BF16)
-        gg[1] = mm(normed, keys_acc[...].astype(BF16), ((0,), (1,))).reshape(qshape).astype(BF16)
-        gg[2] = mm(normed, values_acc[...].astype(BF16), ((0,), (1,))).reshape(qshape).astype(BF16)
+        gg[0] = mm(normed, g_all[1, :, 0:width], TN).reshape(qshape).astype(BF16)
+        gg[1] = mm(normed, keys_acc[...].astype(BF16), TT).reshape(qshape).astype(BF16)
+        gg[2] = mm(normed, values_acc[...].astype(BF16), TT).reshape(qshape).astype(BF16)
         start(gr1)
 
         def grad_first(rows):
             return (
-                mm(dq[rows, :], flat(0), NT)
-                + mm(keys_acc[:, rows].astype(BF16), flat(1), ((0,), (1,)))
-                + mm(values_acc[:, rows].astype(BF16), flat(2), ((0,), (1,)))
+                mm(g_all[1, rows, 0:width], flat(0), NT)
+                + mm(keys_acc[:, rows].astype(BF16), flat(1), TT)
+                + mm(values_acc[:, rows].astype(BF16), flat(2), TT)
             )
 
         def first_back_sib(b, carry):
-            gfirst_s[blk_rows(b), :] = grad_first(sib_rows(b)).astype(BF16)
+            pair_s[0, blk_rows(b), :] = grad_first(sib_rows(b)).astype(BF16)
             return carry
 
         def first_back_own(b, carry):
-            mix[blk_rows(b), :] = grad_first(own_rows(b))
+            gsec[0, blk_rows(b), :] = grad_first(own_rows(b))
             return carry
 
         lax.fori_loop(0, own_blocks, first_back_sib, 0)
         send_first.start()
         lax.fori_loop(0, own_blocks, first_back_own, 0)
 
-    send_first = rcopy(gfirst_s, gfirst_r, sib_ss.at[3], sib_rs.at[3], sib)
     pl.run_scoped(
         last_part,
         pltpu.VMEM(pshape, BF16),
         pltpu.VMEM((width, rows_all), F32),
         pltpu.VMEM((width, rows_all), F32),
-        pltpu.VMEM((rows_all, width), BF16),
     )
 
     arrive(gr1)
-    gg[0:2, :, y] = (gg[0:2, :, y].astype(F32) + q1[0].astype(F32)).astype(BF16)
-    gg[2:4, :, :, x] = (gg[2:4, :, :, x].astype(F32) + q1[1].astype(F32)).astype(BF16)
+    gg[0:2, :, y] = add_low(gg[0:2, :, y], q1[0])
+    gg[2:4, :, :, x] = add_low(gg[2:4, :, :, x], q1[1])
     start(gr2)
-
     send_first.wait_recv()
 
     def back_first(b, carry):
         gain_sum, bias_sum = carry
         r = blk_rows(b)
-        upstream = mix[r, :] + gfirst_r[r, :].astype(F32)
+        upstream = gsec[0, r, :] + gfirst_r[r, :].astype(F32)
         unit, inv_std = row_stats(x_ref[r, :].astype(F32))
-        igrad_ref[r, :] = gm_own[r, :] + row_back(upstream, unit, inv_std, gain1)
+        igrad_ref[r, :] += row_back(upstream, unit, inv_std, gain1)
         gain_sum = gain_sum + jnp.sum(upstream * unit, axis=0, keepdims=True)
         bias_sum = bias_sum + jnp.sum(upstream, axis=0, keepdims=True)
         return gain_sum, bias_sum
 
     gain1_grad, bias1_grad = lax.fori_loop(0, own_blocks, back_first, (zero_row, zero_row))
-    ar_s[0, 0:1, :] = gain1_grad
-    ar_s[0, 1:2, :] = bias1_grad
+    la_s[0] = jnp.zeros(la_s.shape[1:], F32)
+    la_s[0, 0:1, :] = gain1_grad
+    la_s[0, 1:2, :] = bias1_grad
 
     arrive(gr2)
-    gg[0:2, :, y, x] = (gg[0:2, :, y, x].astype(F32) + q2[0].astype(F32)).astype(BF16)
-    gg[2:4, :, y, x] = (gg[2:4, :, y, x].astype(F32) + q2[1].astype(F32)).astype(BF16)
+    gg[0:2, :, y, x] = add_low(gg[0:2, :, y, x], q2[0])
+    gg[2:4, :, y, x] = add_low(gg[2:4, :, y, x], q2[1])
     start(gr3)
 
-    def sum_all(src, dst, ss, rs):
-        for i, peer in enumerate([sib, xn, yn]):
-            c = rcopy(src.at[i], dst.at[i], ss.at[i], rs.at[i], peer)
-            c.start()
-            c.wait()
-            src[i + 1] = src[i] + dst[i]
-        dst[3 + z] = src[3]
-        copies = [
-            rcopy(src.at[3], dst.at[3 + z], ss.at[3 + k], rs.at[3 + k], zn[k]) for k in range(3)
-        ]
-        start(copies)
-        for c in copies:
-            c.wait()
-        return dst[3] + dst[4] + dst[5] + dst[6]
-
-    small = sum_all(ar_s, ar_r, ar_ss, ar_rs)
-    small_ref[...] = small
+    send_mix.wait_recv()
+    back_copies[1].wait_recv()
+
+    def write_out(b, carry):
+        r = blk_rows(b)
+        rows = own_rows(b)
+        out_ref[r, :] = (
+            mid[rows, :]
+            + mix[0, rows, :]
+            + mix_r[r, :].astype(F32)
+            + back_r[1, r, :].astype(F32)
+        )
+        return carry
+
+    lax.fori_loop(0, own_blocks, write_out, 0)
+    rs_e(2)
+    rs_e(3)
 
     arrive(gr3)
     total = gg[:, z, y, x].astype(F32)
@@ -835,37 +1066,44 @@
             acc = acc + jnp.sum(red_ref[a, e] * red_ref[a, e])
         return acc
 
-    share = 1.0 / (2 * GRID_Z * GRID_Y * GRID_X)
     local_sum = lax.fori_loop(0, experts, squares, jnp.sum(total * total))
-    local_sum = local_sum + share * jnp.sum(small * small)
-    sc_s[0] = jnp.full(sc_s.shape[1:], local_sum, F32)
-    sumsq_ref[...] = sum_all(sc_s, sc_r, sc_ss, sc_rs)
+    la_s[0, 2:3, :] = jnp.full((1, D), local_sum, F32)
+    late.one()
+    late.two()
+    late_ref[...] = late.three()
 
     sent(gq1 + gq2 + gq3 + gr1 + gr2 + gr3)
-
-    def drain(e, carry):
-        sent(rs1(e) + rs2(e) + rs3(e))
-        return carry
-
-    lax.fori_loop(0, experts, drain, 0)
-    for c in [send_x, send_g, send_mix, send_first]:
-        c.wait_send()
+    early.done()
+    late.done()
+    sent([send_x, send_g, near_g, near_gates, send_mix, send_first] + back_copies)
+    for i in range(local):
+        sent(ag0(i) + ag1(i) + ag2(i) + ag3(i))
+        sent(rs1(i) + rs2(i) + rs3(i) + rs4(i))
 
     def drain_rows(b, carry):
         gs_copy(b).wait_send()
         return carry
 
+    def drain_own(b, carry):
+        near_x2(b).wait_send()
+        pass_x2(b).wait_send()
+        return carry
+
     lax.fori_loop(0, blocks, drain_rows, 0)
+    lax.fori_loop(0, own_blocks, drain_own, 0)
 
 
 def step_call(x_rows, cotangent, task_ids, routes, norms, qkv, wo, router, win, wout):
     half = x_rows.shape[0]
     rows_all = 2 * half
     experts, shard, hidden = win.shape
+    local = experts // 2
     width = wo.shape[1]
     blocks = rows_all // ROW_BLOCK
+    own_blocks = half // ROW_BLOCK
     heads = width // HD
     vmem = pl.BlockSpec(memory_space=pltpu.VMEM)
+    hbm = pl.BlockSpec(memory_space=pl.ANY)
     grid = (GRID_Z, GRID_Y, GRID_X)
     struct = jax.ShapeDtypeStruct
     dma = pltpu.SemaphoreType.DMA
@@ -875,12 +1113,12 @@
         struct((2, experts, shard, hidden), F32),
         struct((4, shard, width), F32),
         struct((24, D), F32),
-        struct((8, 128), F32),
+        struct((8, D), F32),
         struct((blocks, heads, ROW_BLOCK, rows_all), BF16),
     )
     scratch = [
         pltpu.VMEM((half, D), BF16),
-        pltpu.VMEM((rows_all, D), BF16),
+        pltpu.VMEM((2, rows_all, D), BF16),
         pltpu.VMEM((rows_all, D), BF16),
         pltpu.VMEM((rows_all, width), BF16),
         pltpu.VMEM((rows_all, width), BF16),
@@ -889,63 +1127,166 @@
         pltpu.VMEM((rows_all, D), BF16),
         pltpu.VMEM((rows_all, D), BF16),
         pltpu.VMEM((rows_all, D), F32),
-        pltpu.VMEM((rows_all, D), BF16),
-        pltpu.VMEM((rows_all, experts), F32),
-        pltpu.VMEM((rows_all, experts), F32),
-        pltpu.VMEM((rows_all, D), F32),
-        pltpu.VMEM((rows_all, D), F32),
+        pltpu.VMEM((2, rows_all, D), BF16),
+        pltpu.VMEM((2, 2 * experts, rows_all), F32),
+        pltpu.VMEM((2, experts, rows_all), F32),
+        pltpu.VMEM((2, rows_all, D), F32),
+        pltpu.VMEM((2, rows_all, D), F32),
         pltpu.VMEM((rows_all, D), BF16),
         pltpu.VMEM((half, D), BF16),
         pltpu.VMEM((half, D), BF16),
-        pltpu.VMEM((half, D), F32),
-        pltpu.VMEM((rows_all, D), BF16),
         pltpu.VMEM((rows_all, width), BF16),
         pltpu.VMEM((half, D), BF16),
-        pltpu.VMEM((half, D), BF16),
-        pltpu.VMEM((2, experts) + grid + (shard, hidden), BF16),
-        pltpu.VMEM((experts, 2, 4, 2, shard, hidden), BF16),
-        pltpu.VMEM((experts, 2, 4, shard, hidden), BF16),
-        pltpu.VMEM((experts, 3, 2, shard, hidden), BF16),
+        pltpu.VMEM((2, half, D), BF16),
+        pltpu.VMEM((2, half, D), BF16),
+        pltpu.VMEM((2, half, D), BF16),
+        pltpu.VMEM((2, local) + grid + (shard, hidden), BF16),
+        pltpu.VMEM((2, local) + grid + (shard, hidden), BF16),
+        pltpu.VMEM((2, local, shard, hidden), BF16),
+        pltpu.VMEM((local, 2, 4, 2, shard, hidden), BF16),
+        pltpu.VMEM((local, 2, 4, shard, hidden), BF16),
+        pltpu.VMEM((local, 2, 2, shard, hidden), BF16),
+        pltpu.VMEM((local, 2, shard, hidden), BF16),
         pltpu.VMEM((4,) + grid + (shard, width), BF16),
         pltpu.VMEM((4,) + grid + (shard, width), BF16),
         pltpu.VMEM((2, 2, 4, 2, shard, width), BF16),
         pltpu.VMEM((2, 2, 4, shard, width), BF16),
         pltpu.VMEM((3, 4, shard, width), BF16),
+        pltpu.VMEM((2, 24, D), F32),
+        pltpu.VMEM((8, 24, D), F32),
         pltpu.VMEM((4, 24, D), F32),
-        pltpu.VMEM((7, 24, D), F32),
-        pltpu.VMEM((4, 8, 128), F32),
-        pltpu.VMEM((7, 8, 128), F32),
-        dma((experts, 7)),
-        dma((experts, 7)),
-        dma((experts, 7)),
-        dma((experts, 7)),
-        dma((7,)),
-        dma((7,)),
-        dma((7,)),
-        dma((7,)),
-        dma((4,)),
-        dma((4,)),
-        dma((blocks,)),
-        dma((blocks,)),
-        dma((blocks,)),
-        dma((blocks,)),
-        dma((6,)),
-        dma((6,)),
-        dma((6,)),
-        dma((6,)),
-        dma((2,)),
+        pltpu.VMEM((2, 8, D), F32),
+        pltpu.VMEM((8, 8, D), F32),
+        pltpu.VMEM((4, 8, D), F32),
     ]
+    for size in [
+        (local, 6),
+        (local, 6),
+        (7,),
+        (7,),
+        (7,),
+        (4,),
+        (own_blocks,),
+        (own_blocks,),
+        (blocks,),
+        (blocks,),
+        (10,),
+        (10,),
+    ]:
+        scratch += [dma(size), dma(size)]
+    scratch += [dma((2,)), dma((3,))]
     return pl.pallas_call(
         step_kernel,
         out_shape=outs,
-        in_specs=[vmem, vmem, pl.BlockSpec(memory_space=pltpu.SMEM)] + [vmem] * 7,
-        out_specs=[vmem] * 6 + [pl.BlockSpec(memory_space=pl.ANY)],
+        in_specs=[vmem, hbm, pl.BlockSpec(memory_space=pltpu.SMEM)] + [vmem] * 5 + [hbm] * 2,
+        out_specs=[vmem] * 6 + [hbm],
         scratch_shapes=scratch,
         compiler_params=pltpu.CompilerParams(
             collective_id=0, has_side_effects=True, vmem_limit_bytes=64 << 20
         ),
         name="step",
-    )(x_rows, cotangent, task_ids, routes, norms, qkv, wo, router, win, wout)
+    )(
+        x_rows,
+        cotangent,
+        task_ids,
+        routes.T,
+        norms,
+        qkv,
+        wo,
+        router.T,
+        win,
+        wout,
+    )
+
+
+def adam_parts(weight, first, second, average, gradient, clip_scale, rate):
+    clipped = clip_scale * gradient
+    first_new = BETA_FIRST * first + (1.0 - BETA_FIRST) * clipped
+    second_new = BETA_SECOND * second + (1.0 - BETA_SECOND) * clipped * clipped
+    first_hat = first_new * (1.0 / (1.0 - BETA_FIRST**STEP))
+    second_hat = second_new * (1.0 / (1.0 - BETA_SECOND**STEP))
+    weight_new = weight - rate * (
+        first_hat / (jnp.sqrt(second_hat) + ADAM_EPS) + WEIGHT_DECAY * weight
+    )
+    return weight_new, first_new, second_new, EMA_KEEP * average + (1.0 - EMA_KEEP) * weight_new
+
+
+def adam_kernel(*refs):
+    red, redq, small, late, rows_in, back_in = refs[:6]
+    state = [refs[6 + 4 * k : 10 + 4 * k] for k in range(6)]
+    norm_out, rows_out, back_out = refs[30:33]
+    fresh = [refs[33 + 4 * k : 37 + 4 * k] for k in range(6)]
+    step = pl.program_id(0)
+
+    rows_out[...] = rows_in[...]
+    back_out[...] = back_in[...]
+    norm_grad = jnp.concatenate([late[0:2, :], small[2:4, :]], axis=0)
+    router_grad = small[8:16, :]
+    task_grad = small[16:24, 0:TASKS]
+    total = (
+        jnp.max(late[2:3, 0:1])
+        + jnp.sum(norm_grad * norm_grad)
+        + jnp.sum(router_grad * router_grad)
+        + jnp.sum(task_grad * task_grad)
+    )
+    grad_norm = jnp.sqrt(jnp.full((1, 1), total, F32))
+    clip = jnp.minimum(1.0, CLIP_LIMIT / (grad_norm + 1e-06))
+
+    def update(k, gradient, rate, *index):
+        new = adam_parts(*[r[index] for r in state[k]], gradient, clip, rate)
+        for r, v in zip(fresh[k], new):
+            r[index] = v
+
+    @pl.when(step == 0)
+    def _():
+        norm_out[0] = jnp.max(grad_norm)
+        update(0, norm_grad, NORM_RATE, slice(None))
+        for c in range(3):
+            update(1, redq[c], LEARN_RATE, c)
+        update(2, redq[3], LEARN_RATE, slice(None))
+        update(3, router_grad, LEARN_RATE, slice(None), slice(0, D))
+        update(3, task_grad, LEARN_RATE, slice(None), slice(D, D + TASKS))
+
+    update(4, red[0], LEARN_RATE, slice(None))
+    update(5, red[1], LEARN_RATE, slice(None))
+
+
+def adam_call(red, redq, small, late, output, input_grad, state):
+    experts, shard, hidden = red.shape[1:]
+    per = 2
+    steps = experts // per
+
+    def fixed(array):
+        rank = len(array.shape)
+        return pl.BlockSpec(array.shape, lambda s: (0,) * rank)
+
+    rows = pl.BlockSpec((output.shape[0] // steps, D), lambda s: (s, 0))
+    tile = pl.BlockSpec((per, shard, hidden), lambda s: (s, 0, 0))
+    specs = []
+    for k, group in enumerate(state):
+        specs += [tile if k >= 4 else fixed(a) for a in group]
+    flat = [a for group in state for a in group]
+    struct = jax.ShapeDtypeStruct
+    results = pl.pallas_call(
+        adam_kernel,
+        grid=(steps,),
+        out_shape=[struct((1,), F32), struct(output.shape, F32), struct(output.shape, F32)]
+        + [struct(a.shape, F32) for a in flat],
+        in_specs=[
+            pl.BlockSpec((2, per, shard, hidden), lambda s: (0, s, 0, 0)),
+            fixed(redq),
+            fixed(small),
+            fixed(late),
+            rows,
+            rows,
+        ]
+        + specs,
+        out_specs=[pl.BlockSpec(memory_space=pltpu.SMEM), rows, rows] + specs,
+        compiler_params=pltpu.CompilerParams(vmem_limit_bytes=64 << 20),
+        name="adam",
+    )(red, redq, small, late, output, input_grad, *flat)
+    fresh = [results[3 + 4 * k : 7 + 4 * k] for k in range(6)]
+    return results[0], results[1], results[2], fresh
 
 
 def shards(
@@ -1237,7 +1578,7 @@
     expert_out_second,
     expert_out_ema,
 ):
-    output, input_grad, expert_red, qkvo_red, small, squares, unused = step_call(
+    output, input_grad, expert_red, qkvo_red, small, late, unused = step_call(
         x_rows,
         cotangent,
         task_ids,
@@ -1249,72 +1590,20 @@
         expert_in,
         expert_out,
     )
-    in_reduced, eout_reduced = expert_red[0], expert_red[1]
-    qkv_reduced, out_reduced = qkvo_red[0:3], qkvo_red[3]
-    norm_grad = small[0:4]
-    router_grad = jnp.concatenate([small[8:16].T, small[16:24, 0:TASKS].T], axis=0)
-    total_squares = squares[0, 0]
-    grad_norm = jnp.sqrt(total_squares)
-    clip_scale = jnp.minimum(1.0, CLIP_LIMIT / (grad_norm + 1e-06))
-    norm_new, norm_first_new, norm_second_new, norm_ema_new = adam_update(
-        norm_params, norm_first, norm_second, norm_ema, norm_grad, clip_scale, NORM_RATE
-    )
-    qkv_new, qkv_first_new, qkv_second_new, qkv_ema_new = adam_update(
-        qkv_weight, qkv_first, qkv_second, qkv_ema, qkv_reduced, clip_scale, LEARN_RATE
-    )
-    out_new, out_first_new, out_second_new, out_ema_new = adam_update(
-        out_weight, out_first, out_second, out_ema, out_reduced, clip_scale, LEARN_RATE
-    )
-    router_new, router_first_new, router_second_new, router_ema_new = adam_update(
-        router, router_first, router_second, router_ema, router_grad, clip_scale, LEARN_RATE
-    )
-    in_new, in_first_new, in_second_new, in_ema_new = adam_update(
-        expert_in,
-        expert_in_first,
-        expert_in_second,
-        expert_in_ema,
-        in_reduced,
-        clip_scale,
-        LEARN_RATE,
-    )
-    eout_new, eout_first_new, eout_second_new, eout_ema_new = adam_update(
-        expert_out,
-        expert_out_first,
-        expert_out_second,
-        expert_out_ema,
-        eout_reduced,
-        clip_scale,
-        LEARN_RATE,
-    )
-    return (
-        output,
-        input_grad,
-        grad_norm.reshape(1),
-        norm_new,
-        norm_first_new,
-        norm_second_new,
-        norm_ema_new,
-        qkv_new,
-        qkv_first_new,
-        qkv_second_new,
-        qkv_ema_new,
-        out_new,
-        out_first_new,
-        out_second_new,
-        out_ema_new,
-        router_new,
-        router_first_new,
-        router_second_new,
-        router_ema_new,
-        in_new,
-        in_first_new,
-        in_second_new,
-        in_ema_new,
-        eout_new,
-        eout_first_new,
-        eout_second_new,
-        eout_ema_new,
-    )
+    state = [
+        (norm_params, norm_first, norm_second, norm_ema),
+        (qkv_weight, qkv_first, qkv_second, qkv_ema),
+        (out_weight, out_first, out_second, out_ema),
+        (router.T, router_first.T, router_second.T, router_ema.T),
+        (expert_in, expert_in_first, expert_in_second, expert_in_ema),
+        (expert_out, expert_out_first, expert_out_second, expert_out_ema),
+    ]
+    grad_norm, output, input_grad, fresh = adam_call(
+        expert_red, qkvo_red, small, late, output, input_grad, state
+    )
+    fresh[3] = [a.T for a in fresh[3]]
+    flat = [a for group in fresh for a in group]
+    return (output, input_grad, grad_norm, *flat)
 
 
 def solution(mesh):

time: 270 us -> 211 us (0.78)
  Pallas kernels: 247 us -> 210 us
  other arithmetic: 11.1 us -> 0 us
  local copies, waits for them, and re-layouts: 8.8 us -> 0 us
    pallas_call x1 -> x2, Pallas kernels: 247 us -> 210 us  [the longest x1 202 us: step_call(): pl.pallas_call(step_kernel, out_shape=outs, in_specs=[vmem, hbm, pl.Block...]
    add x5 -> x0, other arithmetic: 11.1 us -> none  [adam_update(): average_new = EMA_KEEP * average + (1.0 - EMA_KEEP) * weight_new]
    unnamed x10 -> x0, local copies, waits for them, and re-layouts: 6.16 us -> none
where the time goes in v2:
time: 211 us
  Pallas kernels  210 us (100%)
    pallas_call x1, Pallas kernels, step_call(): pl.pallas_call(step_kernel, out_shape=outs, in_specs=[vmem, hbm, pl.Block...  202 us
    pallas_call x1, Pallas kernels, adam_call(): pl.pallas_call(adam_kernel, grid=(steps,), out_shape=[struct((1,), F32),...  7.55 us

profile of v2, /device:TPU:0, one launch (start us, length us, event | category | flops | bytes accessed | tf_op | source)
XLA Modules:
  0.0 211.1 jit_solution(10088186780208634846)
XLA Ops:
  1.3 202.1 %step.1 = (f32[768,384]{1,0:T(8,128)}, f32[768,384]{1,0:T(8,128)}, f32[2,8,24,768]{3,2,1,0:T(8,128)}, f32[4,24,192]{2,1,0:T(8,128)}, f32[24,384]{1,0:T(8,128)}, ...) custom-call(bf16[768,384]{1,0:T(8,128)(2,1)} %x_ref.1, f32[768,384]{1,0:T(8,128)} %cot_ref.1, s32[1]{0:T(128)S(6)} %copy.55.task_ref, ...), custom_call_target="tpu_custom_call" | custom-call | tf_op jit(solution)/shard_map/step/pallas_call | solution.py:1178
  203.4 7.5 %adam.1 = (f32[1]{0:T(128)}, f32[768,384]{1,0:T(8,128)}, f32[768,384]{1,0:T(8,128)}, f32[4,384]{1,0:T(4,128)}, f32[4,384]{1,0:T(4,128)}, /*index=5*/f32[4,384]{1...) custom-call(f32[2,8,24,768]{3,2,1,0:T(8,128)} %get-tuple-element.60., ...), custom_call_target="tpu_custom_call" | custom-call | tf_op jit(solution)/shard_map/adam/pallas_call | solution.py:1270

commit v3 on v2

--- a/solution.py
+++ b/solution.py
@@ -155,6 +155,7 @@
 TT = ((0,), (1,))
 GRID_Z, GRID_Y, GRID_X = 4, 2, 2
 ROW_BLOCK = 256
+EXPERT_BLOCK = 512
 
 
 def mm(left, right, dims=NN):
@@ -222,6 +223,7 @@
     r3,
     r4,
     gq,
+    wq,
     gg,
     q1,
     q2,
@@ -232,6 +234,8 @@
     la_s,
     la_g,
     la_z,
+    sc_s,
+    sc_g,
     ag_ss,
     ag_rs,
     rs_ss,
@@ -256,6 +260,8 @@
     ar_rs,
     la_ss,
     la_rs,
+    sc_ss,
+    sc_rs,
     p_sem,
     in_sem,
 ):
@@ -267,11 +273,18 @@
     hidden_width = gw.shape[-1]
     heads = width // HD
     tb = ROW_BLOCK
+    mb = EXPERT_BLOCK
     blocks = rows_all // tb
     own_blocks = half // tb
     pshape = (2, heads, tb, rows_all)
     wshape = gw.shape[2:]
-    qshape = gg.shape[1:]
+    qshape = gg.shape[0:4] + (width,)
+    low_lanes = slice(0, 2 * width)
+    high_lanes = slice(2 * width, 4 * width)
+
+    def part(c):
+        return slice(c * width, (c + 1) * width)
+
 
     d = lax.axis_index("dp")
     m = lax.axis_index("mp")
@@ -308,9 +321,20 @@
         for c in (0, 1)
         if a + b + c > 0
     ]
-    for peer in plane + zn:
+    everyone = [
+        (
+            zk * 4 + (y + a * (1 - 2 * y)) * 2 + (x + b * (1 - 2 * x)),
+            m + c * (1 - 2 * m),
+        )
+        for k, zk in enumerate([z] + zs)
+        for a in (0, 1)
+        for b in (0, 1)
+        for c in (0, 1)
+        if k + a + b + c > 0
+    ]
+    for peer in everyone:
         pl.semaphore_signal(barrier, inc=1, device_id=peer, device_id_type=MESH)
-    pl.semaphore_wait(barrier, 10)
+    pl.semaphore_wait(barrier, len(everyone))
 
     def rcopy(src, dst, ss, rs, dev):
         return pltpu.make_async_remote_copy(
@@ -421,27 +445,31 @@
         red_ref[:, other + i] = r4[i].astype(F32)
 
     gq1 = [
-        rcopy(gq.at[:, z, y, x], gq.at[:, z, y, x], gq_ss.at[k], gq_rs.at[k], zn[k])
-        for k in range(3)
+        rcopy(gq.at[z, y, x], gq.at[z, y, x], gq_ss.at[k], gq_rs.at[k], zn[k]) for k in range(3)
     ]
+
+    def same(ref, sems, k, peer):
+        return rcopy(ref, ref, sems[0].at[k], sems[1].at[k], peer)
+
+    gq_sems = (gq_ss, gq_rs)
     gq2 = [
-        rcopy(gq.at[0:2, :, y, x], gq.at[0:2, :, y, x], gq_ss.at[3], gq_rs.at[3], xn),
-        rcopy(gq.at[2:4, :, y, x], gq.at[2:4, :, y, x], gq_ss.at[4], gq_rs.at[4], yn),
+        same(gq.at[:, y, x, :, low_lanes], gq_sems, 3, xn),
+        same(gq.at[:, y, x, :, high_lanes], gq_sems, 4, yn),
     ]
     gq3 = [
-        rcopy(gq.at[0:2, :, y], gq.at[0:2, :, y], gq_ss.at[5], gq_rs.at[5], yn),
-        rcopy(gq.at[2:4, :, :, x], gq.at[2:4, :, :, x], gq_ss.at[6], gq_rs.at[6], xn),
+        same(gq.at[:, y, :, :, low_lanes], gq_sems, 5, yn),
+        same(gq.at[:, :, x, :, high_lanes], gq_sems, 6, xn),
     ]
     gr1 = [
-        rcopy(gg.at[0:2, :, 1 - y], q1.at[0], gr_ss.at[0], gr_rs.at[0], yn),
-        rcopy(gg.at[2:4, :, :, 1 - x], q1.at[1], gr_ss.at[1], gr_rs.at[1], xn),
+        rcopy(gg.at[:, 1 - y, :, :, low_lanes], q1.at[0], gr_ss.at[0], gr_rs.at[0], yn),
+        rcopy(gg.at[:, :, 1 - x, :, high_lanes], q1.at[1], gr_ss.at[1], gr_rs.at[1], xn),
     ]
     gr2 = [
-        rcopy(gg.at[0:2, :, y, 1 - x], q2.at[0], gr_ss.at[2], gr_rs.at[2], xn),
-        rcopy(gg.at[2:4, :, 1 - y, x], q2.at[1], gr_ss.at[3], gr_rs.at[3], yn),
+        rcopy(gg.at[:, y, 1 - x, :, low_lanes], q2.at[0], gr_ss.at[2], gr_rs.at[2], xn),
+        rcopy(gg.at[:, 1 - y, x, :, high_lanes], q2.at[1], gr_ss.at[3], gr_rs.at[3], yn),
     ]
     gr3 = [
-        rcopy(gg.at[:, zs[k], y, x], q3.at[k], gr_ss.at[4 + k], gr_rs.at[4 + k], zn[k])
+        rcopy(gg.at[zs[k], y, x], q3.at[k], gr_ss.at[4 + k], gr_rs.at[4 + k], zn[k])
         for k in range(3)
     ]
 
@@ -506,11 +534,16 @@
 
     early = SumAll(ar_s, ar_g, ar_z, ar_ss, ar_rs)
     late = SumAll(la_s, la_g, la_z, la_ss, la_rs)
+    me = d * 2 + m
+    last = [
+        rcopy(sc_s, sc_g.at[me], sc_ss.at[k], sc_rs.at[k], peer)
+        for k, peer in enumerate(everyone)
+    ]
 
     send_x.start()
     for c in range(3):
-        gq[c, z, y, x] = qkv_ref[c].astype(BF16)
-    gq[3, z, y, x] = wo_ref[...].astype(BF16)
+        gq[z, y, x, :, part(c)] = qkv_ref[c].astype(BF16)
+    gq[z, y, x, :, part(3)] = wo_ref[...].astype(BF16)
     start(gq1)
 
     load_in.wait()
@@ -562,8 +595,11 @@
     ag_tick(1)
     arrive(gq3)
 
+    for c in range(4):
+        wq[c] = gq[:, :, :, :, part(c)].reshape(D, width)
+
     def flat(c):
-        return gq[c].reshape(D, width)
+        return wq[c]
 
     def project(b, carry):
         r = blk_rows(b)
@@ -604,11 +640,11 @@
             ctx[r, :] = context
             att_s[r, :] = mm(context, flat(3), NT).astype(BF16)
             att_copy(b).start()
-            @pl.when(b == 3)
+            @pl.when(b == 4)
             def _():
                 near_g.start()
 
-            for t, when in ((2, 0), (3, 2), (4, 4)):
+            for t, when in ((2, 1), (3, 3), (4, 5)):
 
                 @pl.when(b == when)
                 def _(t=t):
@@ -621,7 +657,6 @@
         p_out(blocks - 1).wait()
 
     pl.run_scoped(attention, pltpu.VMEM(pshape, BF16))
-    ag_tick(5)
 
     router_t = router_ref[:, 0:D]
     router_hi = router_t.astype(BF16)
@@ -731,21 +766,25 @@
         pair_task = gates[1, experts : experts + 1, 0:128]
         ar_s[0, 16:24, 0:128] = jnp.where(task_row == pair_task, tg, 0.0)
 
-    def pair_rows_back():
-        arrive(pair_copies)
+    def pair_grads_back():
+        pair_copies[0].wait_recv()
 
         def grads(b, carry):
             r = blk_rows(b)
             x_sib[r, :] = (gsec[1, own_rows(b), :] + pair_r[0, r, :].astype(F32)).astype(BF16)
             return carry
 
+        lax.fori_loop(0, own_blocks, grads, 0)
+        back_copies[0].start()
+
+    def pair_mix_back():
+        pair_copies[1].wait_recv()
+
         def rows(b, carry):
             r = blk_rows(b)
             mix_s[r, :] = (mix[1, own_rows(b), :] + pair_r[1, r, :].astype(F32)).astype(BF16)
             return carry
 
-        lax.fori_loop(0, own_blocks, grads, 0)
-        back_copies[0].start()
         lax.fori_loop(0, own_blocks, rows, 0)
         back_copies[1].start()
 
@@ -763,6 +802,7 @@
 
             @pl.when(s == 1)
             def _():
+                ag_tick(5)
                 near_g.wait_recv()
                 pass_g.start()
                 lax.fori_loop(0, own_blocks, pass_rows, 0)
@@ -793,12 +833,11 @@
 
             @pl.when(s == 7)
             def _():
-                pair_rows_back()
                 start(rs1(2))
                 rs_d(1)
 
             def block(b, carry2):
-                r = blk_rows(b)
+                r = pl.ds(pl.multiple_of(b * mb, mb), mb)
                 w_in = gw[0, i].reshape(D, hidden_width)
                 w_out = gw[1, i].reshape(D, hidden_width)
                 gate = gates[st, pl.ds(e, 1), r].T
@@ -819,7 +858,12 @@
                 gsec[st, r, :] += mm(grad_pre, w_in, NT)
                 return carry2
 
-            lax.fori_loop(0, blocks, block, 0)
+            lax.fori_loop(0, rows_all // mb, block, 0)
+
+            @pl.when(s == 6)
+            def _():
+                pair_grads_back()
+
 
             def keep_sum(a, value):
                 @pl.when(first)
@@ -921,7 +965,7 @@
     ar_s[0, 3:4, :] = bias2_grad
     early.one()
     lax.fori_loop(0, own_blocks, back_sib, 0)
-    gg[3] = mm(gml[...], ctx[...], TN).reshape(qshape).astype(BF16)
+    gg[:, :, :, :, part(3)] = mm(gml[...], ctx[...], TN).reshape(qshape).astype(BF16)
 
     pass_g.wait_send()
 
@@ -962,13 +1006,17 @@
                 rs_b(3)
                 rs_c(2)
 
-            @pl.when(b == 2)
+            @pl.when(b == 1)
+            def _():
+                pair_mix_back()
+
+            @pl.when(b == 3)
             def _():
                 rs_c(3)
                 rs_d(2)
                 early.two()
 
-            @pl.when(b == 4)
+            @pl.when(b == 5)
             def _():
                 rs_d(3)
                 rs_e(0)
@@ -980,9 +1028,9 @@
         lax.fori_loop(0, blocks, attend_back, 0)
 
         normed = x1[...]
-        gg[0] = mm(normed, g_all[1, :, 0:width], TN).reshape(qshape).astype(BF16)
-        gg[1] = mm(normed, keys_acc[...].astype(BF16), TT).reshape(qshape).astype(BF16)
-        gg[2] = mm(normed, values_acc[...].astype(BF16), TT).reshape(qshape).astype(BF16)
+        gg[:, :, :, :, part(0)] = mm(normed, g_all[1, :, 0:width], TN).reshape(qshape).astype(BF16)
+        gg[:, :, :, :, part(1)] = mm(normed, keys_acc[...].astype(BF16), TT).reshape(qshape).astype(BF16)
+        gg[:, :, :, :, part(2)] = mm(normed, values_acc[...].astype(BF16), TT).reshape(qshape).astype(BF16)
         start(gr1)
 
         def grad_first(rows):
@@ -1012,8 +1060,8 @@
     )
 
     arrive(gr1)
-    gg[0:2, :, y] = add_low(gg[0:2, :, y], q1[0])
-    gg[2:4, :, :, x] = add_low(gg[2:4, :, :, x], q1[1])
+    gg[:, y, :, :, low_lanes] = add_low(gg[:, y, :, :, low_lanes], q1[0])
+    gg[:, :, x, :, high_lanes] = add_low(gg[:, :, x, :, high_lanes], q1[1])
     start(gr2)
     send_first.wait_recv()
 
@@ -1032,10 +1080,7 @@
     la_s[0, 0:1, :] = gain1_grad
     la_s[0, 1:2, :] = bias1_grad
 
-    arrive(gr2)
-    gg[0:2, :, y, x] = add_low(gg[0:2, :, y, x], q2[0])
-    gg[2:4, :, y, x] = add_low(gg[2:4, :, y, x], q2[1])
-    start(gr3)
+    late.one()
 
     send_mix.wait_recv()
     back_copies[1].wait_recv()
@@ -1052,29 +1097,42 @@
         return carry
 
     lax.fori_loop(0, own_blocks, write_out, 0)
+
+    arrive(gr2)
+    gg[:, y, x, :, low_lanes] = add_low(gg[:, y, x, :, low_lanes], q2[0])
+    gg[:, y, x, :, high_lanes] = add_low(gg[:, y, x, :, high_lanes], q2[1])
+    start(gr3)
     rs_e(2)
     rs_e(3)
 
+    def squares(e, acc):
+        for a in range(2):
+            acc = acc + jnp.sum(red_ref[a, e] * red_ref[a, e], axis=0, keepdims=True)
+        return acc
+
+    columns = lax.fori_loop(0, experts, squares, jnp.zeros((1, hidden_width), F32))
+    late.two()
+
     arrive(gr3)
-    total = gg[:, z, y, x].astype(F32)
+    total = gg[z, y, x].astype(F32)
     for k in range(3):
         total = total + q3[k].astype(F32)
     redq_ref[...] = total
-
-    def squares(e, acc):
-        for a in range(2):
-            acc = acc + jnp.sum(red_ref[a, e] * red_ref[a, e])
-        return acc
-
-    local_sum = lax.fori_loop(0, experts, squares, jnp.sum(total * total))
-    la_s[0, 2:3, :] = jnp.full((1, D), local_sum, F32)
-    late.one()
-    late.two()
-    late_ref[...] = late.three()
+    columns = columns + jnp.sum(total * total, axis=0, keepdims=True)
+    sc_s[...] = jnp.full(sc_s.shape, jnp.sum(columns), F32)
+    start(last)
+    sc_g[me] = sc_s[...]
+    late_ref[0:2, :] = late.three()[0:2]
+    arrive(last)
+    total = sc_g[0]
+    for k in range(1, len(everyone) + 1):
+        total = total + sc_g[k]
+    late_ref[2:8, :] = jnp.broadcast_to(total[0:1, 0:1], (6, D))
 
     sent(gq1 + gq2 + gq3 + gr1 + gr2 + gr3)
     early.done()
     late.done()
+    sent(last)
     sent([send_x, send_g, near_g, near_gates, send_mix, send_first] + back_copies)
     for i in range(local):
         sent(ag0(i) + ag1(i) + ag2(i) + ag3(i))
@@ -1111,7 +1169,7 @@
         struct((half, D), F32),
         struct((half, D), F32),
         struct((2, experts, shard, hidden), F32),
-        struct((4, shard, width), F32),
+        struct((shard, 4 * width), F32),
         struct((24, D), F32),
         struct((8, D), F32),
         struct((blocks, heads, ROW_BLOCK, rows_all), BF16),
@@ -1147,17 +1205,20 @@
         pltpu.VMEM((local, 2, 4, shard, hidden), BF16),
         pltpu.VMEM((local, 2, 2, shard, hidden), BF16),
         pltpu.VMEM((local, 2, shard, hidden), BF16),
-        pltpu.VMEM((4,) + grid + (shard, width), BF16),
-        pltpu.VMEM((4,) + grid + (shard, width), BF16),
-        pltpu.VMEM((2, 2, 4, 2, shard, width), BF16),
-        pltpu.VMEM((2, 2, 4, shard, width), BF16),
-        pltpu.VMEM((3, 4, shard, width), BF16),
+        pltpu.VMEM(grid + (shard, 4 * width), BF16),
+        pltpu.VMEM((4, D, width), BF16),
+        pltpu.VMEM(grid + (shard, 4 * width), BF16),
+        pltpu.VMEM((2, 4, 2, shard, 2 * width), BF16),
+        pltpu.VMEM((2, 4, shard, 2 * width), BF16),
+        pltpu.VMEM((3, shard, 4 * width), BF16),
         pltpu.VMEM((2, 24, D), F32),
         pltpu.VMEM((8, 24, D), F32),
         pltpu.VMEM((4, 24, D), F32),
         pltpu.VMEM((2, 8, D), F32),
         pltpu.VMEM((8, 8, D), F32),
         pltpu.VMEM((4, 8, D), F32),
+        pltpu.VMEM((8, 128), F32),
+        pltpu.VMEM((32, 8, 128), F32),
     ]
     for size in [
         (local, 6),
@@ -1172,6 +1233,7 @@
         (blocks,),
         (10,),
         (10,),
+        (31,),
     ]:
         scratch += [dma(size), dma(size)]
     scratch += [dma((2,)), dma((3,))]
@@ -1217,6 +1279,7 @@
     norm_out, rows_out, back_out = refs[30:33]
     fresh = [refs[33 + 4 * k : 37 + 4 * k] for k in range(6)]
     step = pl.program_id(0)
+    width = redq.shape[1] // 4
 
     rows_out[...] = rows_in[...]
     back_out[...] = back_in[...]
@@ -1242,8 +1305,8 @@
         norm_out[0] = jnp.max(grad_norm)
         update(0, norm_grad, NORM_RATE, slice(None))
         for c in range(3):
-            update(1, redq[c], LEARN_RATE, c)
-        update(2, redq[3], LEARN_RATE, slice(None))
+            update(1, redq[:, c * width : (c + 1) * width], LEARN_RATE, c)
+        update(2, redq[:, 3 * width :], LEARN_RATE, slice(None))
         update(3, router_grad, LEARN_RATE, slice(None), slice(0, D))
         update(3, task_grad, LEARN_RATE, slice(None), slice(D, D + TASKS))
 

time: 211 us -> 201 us (0.953)
  Pallas kernels: 210 us -> 199 us
    pallas_call x1, Pallas kernels: 202 us -> 192 us  [step_call(): pl.pallas_call(step_kernel, out_shape=outs, in_specs=[vmem, hbm, pl.Block...]
where the time goes in v3:
time: 201 us
  Pallas kernels  199 us (99%)
    pallas_call x1, Pallas kernels, step_call(): pl.pallas_call(step_kernel, out_shape=outs, in_specs=[vmem, hbm, pl.Block...  192 us
    pallas_call x1, Pallas kernels, adam_call(): pl.pallas_call(adam_kernel, grid=(steps,), out_shape=[struct((1,), F32),...  7.59 us

profile of v3, /device:TPU:0, one launch (start us, length us, event | category | flops | bytes accessed | tf_op | source)
XLA Modules:
  0.0 200.7 jit_solution(7681147441036037828)
XLA Ops:
  1.3 191.6 %step.1 = (f32[768,384]{1,0:T(8,128)}, f32[768,384]{1,0:T(8,128)}, f32[2,8,24,768]{3,2,1,0:T(8,128)}, f32[24,768]{1,0:T(8,128)}, f32[24,384]{1,0:T(8,128)}, /*in...) custom-call(bf16[768,384]{1,0:T(8,128)(2,1)} %x_ref.1, f32[768,384]{1,0:T(8,128)} %cot_ref.1, s32[1]{0:T(128)S(6)} %copy.55.task_ref, ...), custom_call_target="tpu_custom_call" | custom-call | tf_op jit(solution)/shard_map/step/pallas_call | solution.py:1240
  193.0 7.6 %adam.1 = (f32[1]{0:T(128)}, f32[768,384]{1,0:T(8,128)}, f32[768,384]{1,0:T(8,128)}, f32[4,384]{1,0:T(4,128)}, f32[4,384]{1,0:T(4,128)}, /*index=5*/f32[4,384]{1...) custom-call(f32[2,8,24,768]{3,2,1,0:T(8,128)} %get-tuple-element.60., ...), custom_call_target="tpu_custom_call" | custom-call | tf_op jit(solution)/shard_map/adam/pallas_call | solution.py:1333

commit v4 on v3

--- a/solution.py
+++ b/solution.py
@@ -592,7 +592,15 @@
     load_cot.wait()
     lax.fori_loop(0, own_blocks, cast_cot, 0)
     send_g.start()
-    ag_tick(1)
+    def clear(b, carry):
+        r = blk_rows(b)
+        for st in range(2):
+            mix[st, r, :] = jnp.zeros((tb, D), F32)
+            gsec[st, r, :] = jnp.zeros((tb, D), F32)
+        return carry
+
+    lax.fori_loop(0, blocks, clear, 0)
+    wgt_t[...] = jnp.zeros(wgt_t.shape, F32)
     arrive(gq3)
 
     for c in range(4):
@@ -610,6 +618,8 @@
         return carry
 
     lax.fori_loop(0, blocks, project, 0)
+    ag_tick(1)
+    near_g.start()
 
     def att_copy(b):
         r = blk_rows(b)
@@ -640,15 +650,9 @@
             ctx[r, :] = context
             att_s[r, :] = mm(context, flat(3), NT).astype(BF16)
             att_copy(b).start()
-            @pl.when(b == 4)
+            @pl.when(b == 2)
             def _():
-                near_g.start()
-
-            for t, when in ((2, 1), (3, 3), (4, 5)):
-
-                @pl.when(b == when)
-                def _(t=t):
-                    ag_tick(t)
+                ag_tick(2)
 
             return carry
 
@@ -657,6 +661,8 @@
         p_out(blocks - 1).wait()
 
     pl.run_scoped(attention, pltpu.VMEM(pshape, BF16))
+
+    ag_tick(3)
 
     router_t = router_ref[:, 0:D]
     router_hi = router_t.astype(BF16)
@@ -704,16 +710,6 @@
     near_gates.start()
     send_g.wait_recv()
 
-    def clear(b, carry):
-        r = blk_rows(b)
-        for st in range(2):
-            mix[st, r, :] = jnp.zeros((tb, D), F32)
-            gsec[st, r, :] = jnp.zeros((tb, D), F32)
-        return carry
-
-    lax.fori_loop(0, blocks, clear, 0)
-    wgt_t[...] = jnp.zeros(wgt_t.shape, F32)
-
     def gate_grad(st, share_all, rows):
         share = wgt_t[st, :, rows]
         grad_logits = share - share_all * jnp.sum(share, axis=0, keepdims=True)
@@ -802,14 +798,14 @@
 
             @pl.when(s == 1)
             def _():
-                ag_tick(5)
+                ag_tick(4)
                 near_g.wait_recv()
                 pass_g.start()
-                lax.fori_loop(0, own_blocks, pass_rows, 0)
 
             @pl.when(s == 2)
             def _():
                 pair_rows_in()
+                ag_tick(5)
 
             @pl.when(s == 3)
             def _():
@@ -818,23 +814,23 @@
             @pl.when(s == 4)
             def _():
                 start(rs1(1))
-                rs_b(0)
 
             @pl.when(s == 5)
             def _():
-                rs_b(1)
-                rs_c(0)
+                rs_b(0)
 
             @pl.when(s == 6)
             def _():
                 pair_rows_out()
-                rs_c(1)
-                rs_d(0)
+                rs_b(1)
+                rs_c(0)
+                pair_grads_back()
 
             @pl.when(s == 7)
             def _():
                 start(rs1(2))
-                rs_d(1)
+                rs_c(1)
+                rs_d(0)
 
             def block(b, carry2):
                 r = pl.ds(pl.multiple_of(b * mb, mb), mb)
@@ -860,9 +856,9 @@
 
             lax.fori_loop(0, rows_all // mb, block, 0)
 
-            @pl.when(s == 6)
+            @pl.when(s == 1)
             def _():
-                pair_grads_back()
+                lax.fori_loop(0, own_blocks, pass_rows, 0)
 
 
             def keep_sum(a, value):
@@ -887,7 +883,6 @@
         pltpu.VMEM((rows_all, hidden_width), BF16),
     )
     start(rs1(3))
-    rs_b(2)
 
     def gs_copy(b):
         r = blk_rows(b)
@@ -919,6 +914,9 @@
     ar_s[0, 8:16, :] += rg
     ar_s[0, 16:24, 0:128] += jnp.where(task_row == task.astype(F32), tg, 0.0)
 
+    rs_b(2)
+    rs_d(1)
+    pair_mix_back()
     sent(pair_copies)
 
     def mix_out(b, carry):
@@ -967,6 +965,8 @@
     lax.fori_loop(0, own_blocks, back_sib, 0)
     gg[:, :, :, :, part(3)] = mm(gml[...], ctx[...], TN).reshape(qshape).astype(BF16)
 
+    rs_b(3)
+    rs_c(2)
     pass_g.wait_send()
 
     def last_part(pbuf, keys_acc, values_acc):
@@ -1001,18 +1001,12 @@
                 values_acc[cs, :] += mm(grad_block, prob, TN)
             g_all[1, r, 0:width] = jnp.concatenate(outs, axis=1).astype(BF16)
 
-            @pl.when(b == 0)
+            @pl.when(b == 2)
             def _():
-                rs_b(3)
-                rs_c(2)
-
-            @pl.when(b == 1)
-            def _():
-                pair_mix_back()
+                rs_c(3)
 
             @pl.when(b == 3)
             def _():
-                rs_c(3)
                 rs_d(2)
                 early.two()
 
@@ -1021,7 +1015,6 @@
                 rs_d(3)
                 rs_e(0)
                 rs_e(1)
-                small_ref[...] = early.three()
 
             return carry
 
@@ -1032,6 +1025,7 @@
         gg[:, :, :, :, part(1)] = mm(normed, keys_acc[...].astype(BF16), TT).reshape(qshape).astype(BF16)
         gg[:, :, :, :, part(2)] = mm(normed, values_acc[...].astype(BF16), TT).reshape(qshape).astype(BF16)
         start(gr1)
+        small_ref[...] = early.three()
 
         def grad_first(rows):
             return (

time: 201 us -> 186 us (0.925)
  Pallas kernels: 199 us -> 184 us
    pallas_call x1, Pallas kernels: 192 us -> 177 us  [step_call(): pl.pallas_call(step_kernel, out_shape=outs, in_specs=[vmem, hbm, pl.Block...]
where the time goes in v4:
time: 186 us
  Pallas kernels  184 us (99%)
    pallas_call x1, Pallas kernels, step_call(): pl.pallas_call(step_kernel, out_shape=outs, in_specs=[vmem, hbm, pl.Block...  177 us
    pallas_call x1, Pallas kernels, adam_call(): pl.pallas_call(adam_kernel, grid=(steps,), out_shape=[struct((1,), F32),...  7.59 us

profile of v4, /device:TPU:0, one launch (start us, length us, event | category | flops | bytes accessed | tf_op | source)
XLA Modules:
  0.0 186.0 jit_solution(8238488838643891083)
XLA Ops:
  1.3 176.9 %step.1 = (f32[768,384]{1,0:T(8,128)}, f32[768,384]{1,0:T(8,128)}, f32[2,8,24,768]{3,2,1,0:T(8,128)}, f32[24,768]{1,0:T(8,128)}, f32[24,384]{1,0:T(8,128)}, /*in...) custom-call(bf16[768,384]{1,0:T(8,128)(2,1)} %x_ref.1, f32[768,384]{1,0:T(8,128)} %cot_ref.1, s32[1]{0:T(128)S(6)} %copy.55.task_ref, ...), custom_call_target="tpu_custom_call" | custom-call | tf_op jit(solution)/shard_map/step/pallas_call | solution.py:1234
  178.2 7.6 %adam.1 = (f32[1]{0:T(128)}, f32[768,384]{1,0:T(8,128)}, f32[768,384]{1,0:T(8,128)}, f32[4,384]{1,0:T(4,128)}, f32[4,384]{1,0:T(4,128)}, /*index=5*/f32[4,384]{1...) custom-call(f32[2,8,24,768]{3,2,1,0:T(8,128)} %get-tuple-element.60., ...), custom_call_target="tpu_custom_call" | custom-call | tf_op jit(solution)/shard_map/adam/pallas_call | solution.py:1327

commit v5 on v4

--- a/solution.py
+++ b/solution.py
@@ -1310,7 +1310,7 @@
 
 def adam_call(red, redq, small, late, output, input_grad, state):
     experts, shard, hidden = red.shape[1:]
-    per = 2
+    per = 4
     steps = experts // per
 
     def fixed(array):

time: 186 us -> 185 us (level)
  no operation moved by 1% of the time
where the time goes in v5:
time: 185 us
  Pallas kernels  183 us (99%)
    pallas_call x1, Pallas kernels, step_call(): pl.pallas_call(step_kernel, out_shape=outs, in_specs=[vmem, hbm, pl.Block...  177 us
    pallas_call x1, Pallas kernels, adam_call(): pl.pallas_call(adam_kernel, grid=(steps,), out_shape=[struct((1,), F32),...  6.45 us

profile of v5, /device:TPU:0, one launch (start us, length us, event | category | flops | bytes accessed | tf_op | source)
XLA Modules:
  0.0 184.8 jit_solution(9794673357250253094)
XLA Ops:
  1.3 176.9 %step.1 = (f32[768,384]{1,0:T(8,128)}, f32[768,384]{1,0:T(8,128)}, f32[2,8,24,768]{3,2,1,0:T(8,128)}, f32[24,768]{1,0:T(8,128)}, f32[24,384]{1,0:T(8,128)}, /*in...) custom-call(bf16[768,384]{1,0:T(8,128)(2,1)} %x_ref.1, f32[768,384]{1,0:T(8,128)} %cot_ref.1, s32[1]{0:T(128)S(6)} %copy.55.task_ref, ...), custom_call_target="tpu_custom_call" | custom-call | tf_op jit(solution)/shard_map/step/pallas_call | solution.py:1234
  178.2 6.5 %adam.1 = (f32[1]{0:T(128)}, f32[768,384]{1,0:T(8,128)}, f32[768,384]{1,0:T(8,128)}, f32[4,384]{1,0:T(4,128)}, f32[4,384]{1,0:T(4,128)}, /*index=5*/f32[4,384]{1...) custom-call(f32[2,8,24,768]{3,2,1,0:T(8,128)} %get-tuple-element.60., ...), custom_call_target="tpu_custom_call" | custom-call | tf_op jit(solution)/shard_map/adam/pallas_call | solution.py:1327
